TPU v7x, 256 devices: a whole 4x4x8 slice. The times are simulated.
256 devices in a mesh: depth: 64 (over x, y_lo, z), height: 4 (over y_hi, core).
Axes of the slice: x: 4, y: 4 (y_hi: 2, y_lo: 2; y = y_hi * 2 + y_lo), z: 8, core: 2. Of those that a mesh axis runs over, the one named last changes fastest.
Arguments:
- queries: bfloat16 [14336, 512], P('depth', 'height'), may hold values from -6 to 6
- key_vectors: bfloat16 [14336, 512], P('depth', 'height'), may hold values from -6 to 6
- value_vectors: bfloat16 [14336, 512], P('depth', 'height'), may hold values from -6 to 6
- grad_conv: bfloat16 [128, 16, 56, 256], P('depth', 'height'), may hold values from -6 to 6
- conv_weight: bfloat16 [3, 3, 3, 256, 256], replicated, may hold values from -0.078125 to 0.078125
- dec_weight: bfloat16 [512, 8, 256], replicated, may hold values from -0.125 to 0.125
Outputs:
- grad_queries: bfloat16 [14336, 512], P('depth', 'height')
- grad_keys: bfloat16 [14336, 512], P('depth', 'height')
- grad_values: bfloat16 [14336, 512], P('depth', 'height')
All inputs are finite; a program needn't handle non-finite values.
Results may differ from a plain program's by a relative error of at most 0.024.
Values may be sent and summed in bfloat16 or wider, within the bound.
No kernel may reach another device: no remote copies, remote signals or barrier semaphores. Data moves between devices by JAX's collectives and lax.ppermute only.
A program may use at most 128 MiB of HBM per device.

v0:
```python
import math

import jax
import jax.numpy as jnp
from jax import lax
from jax.sharding import PartitionSpec as P

HSZ = 64


LOSS_SCALE = 64.0
NEG_START = -1e30


def with_halo(block, sides, width):
    for axis, dim in sides:
        count = lax.axis_size(axis)
        forward = [(i, i + 1) for i in range(count - 1)]
        backward = [(target, source) for source, target in forward]
        low = lax.ppermute(
            lax.slice_in_dim(block, block.shape[dim] - width, None, axis=dim), axis, forward
        )
        high = lax.ppermute(lax.slice_in_dim(block, 0, width, axis=dim), axis, backward)
        block = jnp.concatenate([low, block, high], axis=dim)
    return block


def sent_together(arrays, axis, dim, along):
    ends, at = ([], 0)
    for a in arrays[:-1]:
        at += a.shape[along]
        ends.append(at)
    both = jnp.concatenate(arrays, axis=along)
    return tuple(jnp.split(lax.all_gather(both, axis, axis=dim, tiled=True), ends, axis=along))


def rows_first(arrays, axis, dims):
    turned = [jnp.moveaxis(a, dim, 0) for a, dim in zip(arrays, dims)]
    both = jnp.concatenate([t.reshape(len(t), -1) for t in turned], axis=1)
    out, at, done = (lax.all_gather(both, axis, axis=0, tiled=True), 0, [])
    for t, dim in zip(turned, dims):
        section = out[:, at : at + t[0].size].reshape(-1, *t.shape[1:])
        done.append(jnp.moveaxis(section, 0, dim))
        at += t[0].size
    return tuple(done)


def head_scale():
    return 1.0 / math.sqrt(HSZ)


def block_rows(row_count):
    block_size = min(row_count, 2048)
    while row_count % block_size:
        block_size = block_size - 1
    return block_size


def over_blocks(update, carried, pieces):
    row_count = pieces[0].shape[0]
    block_size = block_rows(row_count)
    shaped = tuple(
        (piece.reshape((row_count // block_size, block_size) + piece.shape[1:]) for piece in pieces)
    )

    def advance(current, blocks):
        return (update(current, blocks), None)

    carried, ignored = lax.scan(advance, carried, shaped)
    return carried


def products(left_rows, right_rows):
    left_heads = left_rows.reshape(left_rows.shape[0], -1, HSZ)
    right_heads = right_rows.reshape(right_rows.shape[0], -1, HSZ)
    return jnp.einsum("qhd,khd->hqk", left_heads, right_heads, preferred_element_type=jnp.float32)


def stats_update(queries, grad_rows):

    def update(carried, pieces):
        row_max, denominator, numerator = carried
        key_block, value_block = pieces
        logits = products(queries, key_block) * head_scale()
        new_max = jnp.maximum(row_max, jnp.max(logits, axis=2))
        fading = jnp.exp(row_max - new_max)
        weights = jnp.exp(logits - new_max[:, :, None])
        slopes = products(grad_rows, value_block)
        denominator = denominator * fading + jnp.sum(weights, axis=2)
        numerator = numerator * fading + jnp.sum(weights * slopes, axis=2)
        return (new_max, denominator, numerator)

    return update


def finish_stats(carried):
    row_max, denominator, numerator = carried
    return (row_max + jnp.log(denominator), numerator / denominator)


def softmax_grads(query_rows, grad_rows, log_norm, delta_rows, key_block, value_block):
    logits = products(query_rows, key_block) * head_scale()
    softmax_rows = jnp.exp(logits - log_norm[:, :, None])
    slopes = products(grad_rows, value_block)
    score_grads = (softmax_rows * (slopes - delta_rows[:, :, None])).astype(jnp.bfloat16)
    return (softmax_rows.astype(jnp.bfloat16), score_grads)


def query_term(score_grads, key_block):
    key_heads = key_block.reshape(key_block.shape[0], -1, HSZ)
    result = jnp.einsum("hqk,khd->qhd", score_grads, key_heads, preferred_element_type=jnp.float32)
    return result.reshape(result.shape[0], -1) * head_scale()


def key_term(score_grads, query_rows):
    query_heads = query_rows.reshape(query_rows.shape[0], -1, HSZ)
    result = jnp.einsum(
        "hqk,qhd->khd", score_grads, query_heads, preferred_element_type=jnp.float32
    )
    return result.reshape(result.shape[0], -1) * head_scale()


def value_term(prob_rows, grad_rows):
    grad_heads = grad_rows.reshape(grad_rows.shape[0], -1, HSZ)
    result = jnp.einsum("hqk,qhd->khd", prob_rows, grad_heads, preferred_element_type=jnp.float32)
    return result.reshape(result.shape[0], -1)


def body(queries, key_vectors, value_vectors, grad_conv, conv_weight, dec_weight):
    depth_len, rows_len, cols_len, channels = grad_conv.shape
    padded = with_halo(grad_conv, (("depth", 0), ("height", 1)), 1)
    padded = jnp.pad(padded, ((0, 0), (0, 0), (1, 1), (0, 0)))
    shifted = []
    for along_depth in range(3):
        for along_rows in range(3):
            for along_cols in range(3):
                shifted.append(
                    padded[
                        2 - along_depth : 2 - along_depth + depth_len,
                        2 - along_rows : 2 - along_rows + rows_len,
                        2 - along_cols : 2 - along_cols + cols_len,
                    ]
                )
    stacked = jnp.stack(shifted, axis=3).reshape(depth_len * rows_len * cols_len, 27, channels)
    kernel = conv_weight.reshape(27, channels, channels)
    voxel_grads = lax.dot_general(
        stacked, kernel, (((1, 2), (0, 2)), ((), ())), preferred_element_type=jnp.float32
    )
    voxel_grads = (LOSS_SCALE * voxel_grads).astype(jnp.bfloat16)
    token_rows = rows_len // 2
    token_cols = cols_len // 2
    grouped = voxel_grads.reshape(2, token_rows, 2, token_cols, 2, channels)
    grouped = grouped.transpose(1, 3, 0, 2, 4, 5).reshape(token_rows * token_cols, 8 * channels)
    decoder = dec_weight.reshape(dec_weight.shape[0], 8 * channels)
    out_grads = lax.dot_general(
        grouped, decoder, (((1,), (1,)), ((), ())), preferred_element_type=jnp.float32
    )
    spread = out_grads.astype(jnp.bfloat16).reshape(token_rows, token_cols, decoder.shape[0])
    arranged = lax.all_to_all(spread, "height", split_axis=2, concat_axis=0, tiled=True)
    grad_rows = arranged.reshape(-1, arranged.shape[2])
    tokens_here, width_here = queries.shape
    heads_here = width_here // HSZ
    empty_rows = jnp.zeros((heads_here, tokens_here), jnp.float32)
    start_stats = (
        jnp.full((heads_here, tokens_here), NEG_START, jnp.float32),
        empty_rows,
        empty_rows,
    )
    empty_grads = jnp.zeros((tokens_here, width_here), jnp.float32)
    update = stats_update(queries, grad_rows)
    every_keys, every_values = sent_together((key_vectors, value_vectors), "depth", 0, 1)
    log_norm, delta_rows = finish_stats(
        over_blocks(update, start_stats, (every_keys, every_values))
    )
    every_queries, every_grads = sent_together((queries, grad_rows), "depth", 0, 1)
    every_norms, every_deltas = rows_first((log_norm, delta_rows), "depth", (1, 1))

    def query_update(query_acc, pieces):
        key_block, value_block = pieces
        prob_rows, score_grads = softmax_grads(
            queries, grad_rows, log_norm, delta_rows, key_block, value_block
        )
        return query_acc + query_term(score_grads, key_block)

    query_acc = over_blocks(query_update, empty_grads, (every_keys, every_values))

    def owner_update(carried, pieces):
        key_acc, value_acc = carried
        query_block, grad_block, norm_block, delta_block = pieces
        prob_rows, score_grads = softmax_grads(
            query_block, grad_block, norm_block.T, delta_block.T, key_vectors, value_vectors
        )
        return (
            key_acc + key_term(score_grads, query_block),
            value_acc + value_term(prob_rows, grad_block),
        )

    grad_keys, grad_values = over_blocks(
        owner_update,
        (empty_grads, empty_grads),
        (every_queries, every_grads, every_norms.T, every_deltas.T),
    )
    return (
        query_acc.astype(jnp.bfloat16),
        grad_keys.astype(jnp.bfloat16),
        grad_values.astype(jnp.bfloat16),
    )


def solution(mesh):
    in_specs = (
        P("depth", "height"),
        P("depth", "height"),
        P("depth", "height"),
        P("depth", "height", None, None),
        P(),
        P(),
    )
    out_specs = (P("depth", "height"), P("depth", "height"), P("depth", "height"))
    return jax.shard_map(body, mesh=mesh, in_specs=in_specs, out_specs=out_specs, check_vma=False)
```

profile of v0, /device:TPU:16, one launch (start us, length us, event | category | flops | bytes accessed | tf_op | source)
XLA Modules:
  0.0 732.4 jit_solution(16794380680627807546)
XLA Ops:
  9.9 3.8 collective-permute-start
  16.1 4.3 collective-permute-done.1
  23.5 5.1 collective-permute-start.3
  28.7 3.6 copy.89
  34.0 2.5 fusion.18
  41.6 4.9 all-to-all-start
  51.3 269.0 %all-gather.4.cloned.1.call-done = bf16[14336,256]{1,0:T(8,128)(2,1)} async-done(((bf16[224,256]{1,0:T(8,128)(2,1)}), bf16[14336,256]{1,0:T(8,128)(2,1)}) %all-gather.4.cloned.1.call-update) | async-done | bytes 7340048 | tf_op jit(solution)/shard_map/all_gather | solution.py:34
  320.3 5.2 fusion.29
  325.5 6.1 copy.69
  331.6 6.2 copy.71
  337.9 55.2 %while.39 = (s32[]{:T(128)}, f32[2,224]{1,0:T(2,128)S(1)}, f32[2,224]{1,0:T(2,128)S(1)}, f32[2,224]{1,0:T(2,128)S(1)}, bf16[7,2048,128]{1,2,0:T(8,128)(2,1)}, /*...) while((s32[]{:T(128)}, f32[2,224]{1,0:T(2,128)S(1)}, ...), condition=%wide.region_4.5_spmd.clone, body=%wide.region_0.4_spmd.clone.sunk | while | flops 243141696 | bytes 29097616 | solution.py:69
  341.8 3.2 fusion.82
  349.7 3.2 fusion.82
  357.6 3.2 fusion.82
  365.4 3.2 fusion.82
  373.3 3.2 fusion.82
  381.2 3.2 fusion.82
  389.1 3.2 fusion.82
  393.1 157.2 %all-gather = f32[64,224,4]{1,2,0:T(4,128)S(1)} all-gather(f32[1,224,4]{1,2,0:T(4,128)S(1)} %maximum_bitcast_fusion), channel_id=1, replica_groups=mesh['depth'=64,'height'=4] {'depth'}, dimensions={0}, use_global_device_ids=true | all-gather | bytes 232960 | tf_op jit(solution)/shard_map/all_gather | solution.py:40
  550.6 52.0 %while.40 = (s32[]{:T(128)}, f32[224,128]{0,1:T(8,128)S(1)}, bf16[7,2048,128]{1,2,0:T(8,128)(2,1)}, bf16[224,128]{0,1:T(8,128)(2,1)S(1)}, f32[2,224]{1,0:T(2,128...) while((s32[]{:T(128)}, f32[224,128]{0,1:T(8,128)S(1)}, ...), condition=%wide.region_6.7_spmd.clone, body=%wide.region_5.6_spmd.clone.sunk | while | flops 356995072 | bytes 11701875 | solution.py:69
  554.5 3.5 fusion.91
  562.0 3.5 fusion.91
  569.4 3.5 fusion.91
  576.8 3.5 fusion.91
  584.3 3.5 fusion.91
  591.7 3.5 fusion.91
  599.1 3.5 fusion.91
  603.5 24.8 %all-gather.6.cloned.1.call-done = bf16[14336,256]{1,0:T(8,128)(2,1)} async-done(((bf16[224,256]{1,0:T(8,128)(2,1)}), bf16[14336,256]{1,0:T(8,128)(2,1)}) %all-gather.6.cloned.1.call-update) | async-done | bytes 7340048 | tf_op jit(solution)/shard_map/all_gather | solution.py:34
  628.3 5.2 fusion.28
  633.5 88.6 %while.41 = (s32[]{:T(128)}, f32[224,128]{0,1:T(8,128)}, f32[224,128]{0,1:T(8,128)}, bf16[7,2048,128]{2,1,0:T(8,128)(2,1)}, bf16[224,128]{0,1:T(8,128)(2,1)S(1)}...) while((s32[]{:T(128)}, f32[224,128]{0,1:T(8,128)}, ...), condition=%wide.region_8.9_spmd.clone, body=%wide.region_7.8_spmd.clone.sunk | while | flops 475410432 | bytes 18432132 | solution.py:69
  634.8 2.5 subtract_exponential_fusion.3
  638.6 3.2 fusion.100
  641.9 2.7 fusion.99
  650.5 3.2 fusion.100
  653.7 2.7 fusion.99
  659.5 2.5 subtract_exponential_fusion.3
  663.3 3.2 fusion.100
  666.5 2.7 fusion.99
  672.3 2.5 subtract_exponential_fusion.3
  676.1 3.2 fusion.100
  679.3 2.7 fusion.99
  685.0 2.5 subtract_exponential_fusion.3
  688.8 3.2 fusion.100
  692.1 2.7 fusion.99
  701.6 3.2 fusion.100
  704.9 2.7 fusion.99
  714.4 3.2 fusion.100
  717.7 2.7 fusion.99
  (228 shorter events, 120.5 us)
Async XLA Ops:
  7.2 26.8 %copy-start = (bf16[3,3,3,256,256]{4,3,2,1,0:T(8,128)(2,1)S(1)}, bf16[3,3,3,256,256]{4,3,2,1,0:T(8,128)(2,1)}, u32[]{:S(2)}) copy-start(bf16[3,3,3,256,256]{4,3,2,1,0:T(8,128)(2,1)} %param.16) | copy-start | bytes 10616836
  7.2 313.1 %all-gather.4.cloned.1.call-start = ((), (), s32[]{:S(2)}) async-start(), calls=%async_computation.1 | async-start | bytes 7454720 | tf_op jit(solution)/shard_map/all_gather | solution.py:34
  9.9 6.2 collective-permute-start
  13.7 6.7 collective-permute-start.1
  21.6 10.7 %collective-permute-start.2 = (bf16[4,1,56,256]{3,2,1,0:T(8,128)(2,1)S(1)}, bf16[4,1,56,256]{3,2,1,0:T(8,128)(2,1)S(1)}, u32[]{:S(2)}, u32[]{:S(2)}) collective-permute-start(bf16[4,1,56,256]{3,2,1,0:T(8,128)(2,1)S(1)} %get-tuple-element.410), channel_id=1, source_target_pairs={{0,1},{1,2},{2,3},{4,5},{5,6},{6,7},{8,9},{9,10},{10,11},{12,13},{... | collective-permute-start | bytes 344072 | tf_op jit(solution)/shard_map/ppermute | solution.py:20
  23.5 8.8 %collective-permute-start.3 = (bf16[4,1,56,256]{3,2,1,0:T(8,128)(2,1)S(1)}, bf16[4,1,56,256]{3,2,1,0:T(8,128)(2,1)S(1)}, u32[]{:S(2)}, u32[]{:S(2)}) collective-permute-start(bf16[4,1,56,256]{3,2,1,0:T(8,128)(2,1)S(1)} %get-tuple-element.411), channel_id=1, source_target_pairs={{1,0},{2,1},{3,2},{5,4},{6,5},{7,6},{9,8},{10,9},{11,10},{13,12},{... | collective-permute-start | bytes 344072 | tf_op jit(solution)/shard_map/ppermute | solution.py:23
  32.6 1.0 copy-start.3
  36.5 14.1 %copy-start.4 = (bf16[224,128]{1,0:T(8,128)(2,1)S(1)}, bf16[224,128]{1,0:T(8,128)(2,1)}, u32[]{:S(2)}) copy-start(bf16[224,128]{1,0:T(8,128)(2,1)} %param.12) | copy-start | bytes 172036
  41.6 8.1 %all-to-all-start = ((bf16[4,2,3584]{2,1,0:T(2,128)(2,1)}), bf16[4,2,3584]{2,1,0:T(2,128)(2,1)S(1)}, u32[]{:S(2)}, u32[]{:S(2)}) async-start(bf16[4,2,3584]{2,1,0:T(2,128)(2,1)} %reshape.179), calls=%async_computation | async-start | bytes 114688 | tf_op jit(solution)/shard_map/all_to_all | solution.py:159
  46.5 581.8 %all-gather.6.cloned.1.call-start = ((), (), s32[]{:S(2)}) async-start(), calls=%async_computation.2 | async-start | bytes 7454720 | tf_op jit(solution)/shard_map/all_gather | solution.py:34
  341.8 3.2 copy-start.2
  349.7 3.2 copy-start.2
  357.6 3.2 copy-start.2
  365.4 3.2 copy-start.2
  373.3 3.2 copy-start.2
  381.2 3.2 copy-start.2
  389.1 3.2 copy-start.2
  722.1 3.4 copy-start.1
Sparse Core Ops, SparseCore 0:
  9.8 310.4 all-gather.3
  322.1 306.1 all-gather.5
where the time goes:
time: 735 us; the launch traced here: 732 us
  waiting for transfers between devices  300 us (41%)
  blocking collectives  157 us (21%)
  matrix products  145 us (20%)
  local copies, waits for them, and re-layouts  77.2 us (11%)
  other arithmetic  20.4 us (3%)
  starting transfers between devices  17.1 us (2%)
  between operations  14.5 us (2%)
    all_gather x2, waiting for transfers between devices, sent_together(): lax.all_gather(both, axis, axis=dim, tiled=True)  294 us
    all_gather x1, blocking collectives, rows_first(): out, at, done = (lax.all_gather(both, axis, axis=0, tiled=True), 0, [])  157 us
    dot_general x28, matrix products, products(): jnp.einsum('qhd,khd->hqk', left_heads, right_heads, preferred_element_typ...  74.3 us
    dynamic_slice x42, local copies, waits for them, and re-layouts, over_blocks(): carried, ignored = lax.scan(advance, carried, shaped)  36.3 us
    dot_general x7, matrix products, query_term(): jnp.einsum('hqk,khd->qhd', score_grads, key_heads, preferred_element_type...  24.3 us
    dot_general x7, matrix products, key_term(): jnp.einsum('hqk,qhd->khd', score_grads, query_heads, preferred_element_ty...  22.6 us
    unnamed x45, local copies, waits for them, and re-layouts  21.2 us
    dot_general x7, matrix products, value_term(): jnp.einsum('hqk,qhd->khd', prob_rows, grad_heads, preferred_element_type=...  19.1 us
  transfers between devices with their start and end apart: 7, of which 5 were waited for; matrix products, arithmetic and copies ran while one was open for 20% of the time, Pallas kernels for 0%

commit v1 on v0

v1 whole, which is shorter than its diff:
```python
import math

import jax
import jax.numpy as jnp
from jax import lax
from jax.experimental import pallas as pl
from jax.experimental.pallas import tpu as pltpu
from jax.sharding import Mesh
from jax.sharding import PartitionSpec as P

HSZ = 64
LOSS_SCALE = 64.0
NEG_START = -1e30
HEAD_SCALE = 1.0 / math.sqrt(HSZ)
LOG2_SCALE = math.log2(math.e) / math.sqrt(HSZ)
KEY_AXES = ("x", "y")
QUERY_AXIS = "z"
DEPTH = ("x", "y", "z")
SPAN = 64
TILE = 256


def halo_pair(block, axis, dim):
    count = lax.axis_size(axis)
    forward = [(i, i + 1) for i in range(count - 1)]
    backward = [(target, source) for source, target in forward]
    last = lax.slice_in_dim(block, block.shape[dim] - 1, None, axis=dim)
    low = lax.ppermute(last, axis, forward)
    high = lax.ppermute(lax.slice_in_dim(block, 0, 1, axis=dim), axis, backward)
    return low, high


def product(left, right):
    return lax.dot_general(
        left, right, (((1,), (0,)), ((), ())), preferred_element_type=jnp.float32
    )


def product_t(left, right):
    return lax.dot_general(
        left, right, (((1,), (1,)), ((), ())), preferred_element_type=jnp.float32
    )


def conv_body(
    own_ref, before_ref, after_ref, above_ref, below_ref, w_ref, dec_ref, out_ref, x_ref, acc_ref, vox_ref, tok_ref
):
    step = pl.program_id(0)
    planes, rows, cols, channels = own_ref.shape

    @pl.when(step == 0)
    def _():
        for d in range(planes + 2):
            for r in range(rows + 2):
                if r == 0:
                    row = above_ref[d, 0]
                elif r == rows + 1:
                    row = below_ref[d, 0]
                elif d == 0:
                    row = before_ref[0, r - 1]
                elif d == planes + 1:
                    row = after_ref[0, r - 1]
                else:
                    row = own_ref[d - 1, r - 1]
                row = row.astype(jnp.float32)
                row = jnp.concatenate(
                    [row, jnp.zeros((SPAN - cols, channels), jnp.float32)], axis=0
                )
                x_ref[0, d, r] = pltpu.roll(row, SPAN - 1, 0).astype(jnp.bfloat16)
                x_ref[1, d, r] = row.astype(jnp.bfloat16)
                x_ref[2, d, r] = pltpu.roll(row, 1, 0).astype(jnp.bfloat16)
        acc_ref[...] = jnp.zeros_like(acc_ref)

    along_depth = step // 3
    along_rows = step % 3
    summed = acc_ref[...]
    for tap in range(3):
        window = x_ref[tap, pl.ds(2 - along_depth, planes), pl.ds(2 - along_rows, rows)]
        summed += product_t(window.reshape(planes * rows * SPAN, channels), w_ref[0, 0, tap])
    acc_ref[...] = summed

    @pl.when(step == 8)
    def _():
        voxels = (LOSS_SCALE * summed).astype(jnp.bfloat16).astype(jnp.float32)
        lanes = vox_ref.shape[2]
        for side in range(channels // lanes):
            vox_ref[side] = voxels[:, side * lanes : (side + 1) * lanes]
        half = SPAN // 2
        tokens = None
        for s in range(8):
            a, b, c = s // 4, s // 2 % 2, s % 2
            parts = []
            for h in range(rows // 2):
                at = pl.ds((a * rows + 2 * h + b) * SPAN + c, half, stride=2)
                sides = [vox_ref[side, at, :] for side in range(channels // lanes)]
                parts.append(jnp.concatenate(sides, axis=1))
            part = product_t(
                jnp.concatenate(parts, axis=0).astype(jnp.bfloat16),
                dec_ref[:, s * channels : (s + 1) * channels],
            )
            tokens = part if tokens is None else tokens + part
        for h in range(rows // 2):
            tok_ref[h * (cols // 2) : (h + 1) * (cols // 2), :] = tokens[
                h * half : h * half + cols // 2
            ]
        done = tok_ref[...].astype(jnp.bfloat16)
        copies, heights, _, width = out_ref.shape
        for place in range(copies):
            for height in range(heights):
                out_ref[place, height] = done[:, height * width : (height + 1) * width]


def conv_tokens(own, before, after, above, below, weight, decoder, copies, heights):
    planes, rows, cols, channels = own.shape
    tokens = planes // 2 * (rows // 2) * (cols // 2)
    features = decoder.shape[0]

    def whole(array):
        return pl.BlockSpec(array.shape, lambda t: (0,) * array.ndim)

    out_shape = (copies, heights, tokens, features // heights)
    return pl.pallas_call(
        conv_body,
        grid=(9,),
        in_specs=[
            whole(own),
            whole(before),
            whole(after),
            whole(above),
            whole(below),
            pl.BlockSpec((1, 1, 3, channels, channels), lambda t: (t // 3, t % 3, 0, 0, 0)),
            whole(decoder),
        ],
        out_specs=pl.BlockSpec(out_shape, lambda t: (0, 0, 0, 0)),
        out_shape=jax.ShapeDtypeStruct(out_shape, jnp.bfloat16),
        scratch_shapes=[
            pltpu.VMEM((3, planes + 2, rows + 2, SPAN, channels), jnp.bfloat16),
            pltpu.VMEM((planes * rows * SPAN, channels), jnp.float32),
            pltpu.VMEM((channels // 128, planes * rows * SPAN, 128), jnp.float32),
            pltpu.VMEM((tokens, features), jnp.float32),
        ],
        name="conv",
    )(own, before, after, above, below, weight, decoder)


def own_rows(turned, head):
    rows = lax.broadcasted_iota(jnp.int32, turned.shape, 0) // HSZ
    return jnp.where(rows == head, turned, jnp.zeros_like(turned))


def stats_body(kv_ref, q_ref, g_ref, out_ref, qt_ref, gt_ref, *, rows):
    width = q_ref.shape[1]
    qt = q_ref[...].T
    gt = g_ref[...].T
    qt_ref[...] = qt
    gt_ref[...] = gt
    wide = qt.shape[1]
    for head in range(width // HSZ):
        qh = own_rows(qt, head)
        gh = own_rows(gt, head)

        def step(i, carried):
            top, total, weighted = carried
            at = pl.multiple_of(i * rows, rows)
            logits = product(kv_ref[pl.ds(at, rows), :width], qh).reshape(rows // 8, 8, wide)
            slopes = product(kv_ref[pl.ds(at, rows), width:], gh).reshape(rows // 8, 8, wide)
            new_top = jnp.maximum(top, jnp.max(logits, axis=0))
            fade = jnp.exp2((top - new_top) * LOG2_SCALE)
            weights = jnp.exp2((logits - new_top[None]) * LOG2_SCALE)
            total = total * fade + jnp.sum(weights, axis=0)
            weighted = weighted * fade + jnp.sum(weights * slopes, axis=0)
            return new_top, total, weighted

        zero = jnp.zeros((8, wide), jnp.float32)
        start = (jnp.full((8, wide), NEG_START, jnp.float32), zero, zero)
        top, total, weighted = lax.fori_loop(0, kv_ref.shape[0] // rows, step, start, unroll=True)
        best = jnp.max(top, axis=0, keepdims=True)
        fade = jnp.exp2((top - best) * LOG2_SCALE)
        total = jnp.sum(total * fade, axis=0, keepdims=True)
        weighted = jnp.sum(weighted * fade, axis=0, keepdims=True)
        log_sum = best * LOG2_SCALE + jnp.log2(total)
        delta = weighted / total
        for place in range(out_ref.shape[0]):
            out_ref[place, 2 * head : 2 * head + 1, :] = log_sum
            out_ref[place, 2 * head + 1 : 2 * head + 2, :] = delta


def local_stats(both, queries, grads, copies):
    count, pair = both.shape
    query_count, width = queries.shape
    heads = width // HSZ
    tile = pl.BlockSpec((TILE, width), lambda i: (i, 0))
    turned = pl.BlockSpec((width, TILE), lambda i: (0, i))
    return pl.pallas_call(
        lambda *refs: stats_body(*refs, rows=128),
        grid=(query_count // TILE,),
        in_specs=[pl.BlockSpec((count, pair), lambda i: (0, 0)), tile, tile],
        out_specs=[
            pl.BlockSpec((copies, 2 * heads, TILE), lambda i: (0, 0, i)),
            turned,
            turned,
        ],
        out_shape=[
            jax.ShapeDtypeStruct((copies, 2 * heads, query_count), jnp.float32),
            jax.ShapeDtypeStruct((width, query_count), jnp.bfloat16),
            jax.ShapeDtypeStruct((width, query_count), jnp.bfloat16),
        ],
        name="stats",
    )(both, queries, grads)


def grads_body(
    kv_ref, q_ref, g_ref, qt_ref, gt_ref, part_ref, dkv_ref, dq_ref, p_ref, s_ref, acc_ref, st_ref
):
    block = pl.program_id(0)
    rows = kv_ref.shape[0]
    count, width = q_ref.shape

    @pl.when(block == 0)
    def _():
        for head in range(width // HSZ):
            logs = part_ref[:, 2 * head, :]
            best = jnp.max(logs, axis=0, keepdims=True)
            shares = jnp.exp2(logs - best)
            total = jnp.sum(shares, axis=0, keepdims=True)
            delta = jnp.sum(shares * part_ref[:, 2 * head + 1, :], axis=0, keepdims=True)
            st_ref[2 * head : 2 * head + 1, :] = best + jnp.log2(total)
            st_ref[2 * head + 1 : 2 * head + 2, :] = delta / total
        acc_ref[...] = jnp.zeros_like(acc_ref)

    keys = kv_ref[:, :width]
    values = kv_ref[:, width:]
    keys_t = keys.T
    head_of = lax.broadcasted_iota(jnp.int32, (rows, width), 1) // HSZ
    dks = []
    dvs = []
    for head in range(width // HSZ):
        mine = head_of == head
        head_keys = jnp.where(mine, keys, jnp.zeros_like(keys))
        head_values = jnp.where(mine, values, jnp.zeros_like(values))
        for i in range(count // TILE):
            at = slice(i * TILE, (i + 1) * TILE)
            logits = product(head_keys, qt_ref[:, at])
            slopes = product(head_values, gt_ref[:, at])
            probs = jnp.exp2(logits * LOG2_SCALE - st_ref[2 * head : 2 * head + 1, at])
            p_ref[head, :, at] = probs.astype(jnp.bfloat16)
            s_ref[head, :, at] = (probs * (slopes - st_ref[2 * head + 1 : 2 * head + 2, at])).astype(
                jnp.bfloat16
            )
        dvs.append(product(p_ref[head], g_ref[...]))
        dks.append(product(s_ref[head], q_ref[...]))
        span = slice(head * HSZ, (head + 1) * HSZ)
        acc_ref[span, :] += product(keys_t[span], s_ref[head])
    dk, dv = (dks[-1], dvs[-1])
    for head in range(len(dks) - 1):
        dk = jnp.where(head_of == head, dks[head], dk)
        dv = jnp.where(head_of == head, dvs[head], dv)
    dkv_ref[:, :width] = (dk * HEAD_SCALE).astype(jnp.bfloat16)
    dkv_ref[:, width:] = dv.astype(jnp.bfloat16)

    @pl.when(block == pl.num_programs(0) - 1)
    def _():
        dq_ref[...] = (acc_ref[...] * HEAD_SCALE).T.astype(jnp.bfloat16)


def local_grads(both, queries, grads, queries_t, grads_t, parts):
    count, pair = both.shape
    query_count, width = queries.shape
    heads = width // HSZ
    rows = 256
    block = pl.BlockSpec((rows, pair), lambda i: (i, 0))

    def whole(*shape):
        return pl.BlockSpec(shape, lambda i: (0,) * len(shape))

    return pl.pallas_call(
        grads_body,
        grid=(count // rows,),
        in_specs=[
            block,
            whole(query_count, width),
            whole(query_count, width),
            whole(width, query_count),
            whole(width, query_count),
            whole(*parts.shape),
        ],
        out_specs=[block, whole(query_count, width)],
        out_shape=[
            jax.ShapeDtypeStruct((count, pair), jnp.bfloat16),
            jax.ShapeDtypeStruct((query_count, width), jnp.bfloat16),
        ],
        scratch_shapes=[
            pltpu.VMEM((heads, rows, query_count), jnp.bfloat16),
            pltpu.VMEM((heads, rows, query_count), jnp.bfloat16),
            pltpu.VMEM((width, query_count), jnp.float32),
            pltpu.VMEM((2 * heads, query_count), jnp.float32),
        ],
        name="grads",
    )(both, queries, grads, queries_t, grads_t, parts)


def spread_to(array, axes):
    count = lax.axis_size(axes)
    copies = jnp.broadcast_to(array[None], (count,) + array.shape)
    return lax.all_to_all(copies, axes, 0, 0, tiled=True)


def body(queries, key_vectors, value_vectors, grad_conv, conv_weight, dec_weight):
    tokens, width = queries.shape
    heights = lax.axis_size("height")
    places = lax.axis_size(QUERY_AXIS)
    before, after = halo_pair(grad_conv, DEPTH, 0)
    padded = jnp.concatenate([before, grad_conv, after], axis=0)
    above, below = halo_pair(padded, "height", 1)
    both = spread_to(jnp.concatenate([key_vectors, value_vectors], axis=1), KEY_AXES)
    both = both.reshape(-1, 2 * width)
    every_query = spread_to(queries, QUERY_AXIS).reshape(-1, width)
    decoder = dec_weight.reshape(dec_weight.shape[0], -1)
    apart = conv_tokens(
        grad_conv, before, after, above, below, conv_weight, decoder, places, heights
    )
    apart = apart.reshape((places * heights,) + apart.shape[2:])
    every_grad = lax.all_to_all(apart, (QUERY_AXIS, "height"), 0, 0, tiled=True).reshape(-1, width)
    part, queries_t, grads_t = local_stats(both, every_query, every_grad, places)
    parts = lax.all_to_all(part, QUERY_AXIS, 0, 0, tiled=True)
    dkv, dq = local_grads(both, every_query, every_grad, queries_t, grads_t, parts)
    arrived = lax.all_to_all(dkv.reshape(-1, tokens, 2 * width), KEY_AXES, 0, 0, tiled=True)
    owned = jnp.sum(arrived.astype(jnp.float32), axis=0).astype(jnp.bfloat16)
    dq = lax.all_to_all(dq.reshape(-1, tokens, width), QUERY_AXIS, 0, 0, tiled=True)
    dq = jnp.sum(dq.astype(jnp.float32), axis=0).astype(jnp.bfloat16)
    return dq, owned[:, :width], owned[:, width:]


def solution(mesh):
    fine = Mesh(mesh.devices.reshape(4, 2, 8, 4), ("x", "y", "z", "height"))
    in_specs = (
        P(DEPTH, "height"),
        P(DEPTH, "height"),
        P(DEPTH, "height"),
        P(DEPTH, "height", None, None),
        P(),
        P(),
    )
    out_specs = (P(DEPTH, "height"), P(DEPTH, "height"), P(DEPTH, "height"))
    return jax.shard_map(body, mesh=fine, in_specs=in_specs, out_specs=out_specs, check_vma=False)
```

time: 735 us -> 172 us (0.23)
  waiting for transfers between devices: 300 us -> 32.8 us
  matrix products: 145 us -> 0 us
  blocking collectives: 157 us -> 56 us
  local copies, waits for them, and re-layouts: 77.2 us -> 8.79 us
  Pallas kernels: 0 us -> 40.1 us
  other arithmetic: 20.4 us -> 1.72 us
  between operations: 14.5 us -> 0.75 us
  starting transfers between devices: 17.1 us -> 29.9 us
    all_gather x2 -> x0, waiting for transfers between devices: 294 us -> none  [sent_together(): lax.all_gather(both, axis, axis=dim, tiled=True)]
    all_gather x1 -> x0, blocking collectives: 157 us -> none  [rows_first(): out, at, done = (lax.all_gather(both, axis, axis=0, tiled=True), 0, [])]
    dot_general x51 -> x0, matrix products: 145 us -> none  [the longest x28 74.3 us: products(): jnp.einsum('qhd,khd->hqk', left_heads, right_heads, preferred_element_typ...]
    all_to_all x0 -> x3, blocking collectives: none -> 56 us  [the longest x1 25.3 us: body(): lax.all_to_all(apart, (QUERY_AXIS, 'height'), 0, 0, tiled=True)]
    pallas_call x0 -> x3, Pallas kernels: none -> 40.1 us  [the longest x1 19.2 us: local_grads(): pl.pallas_call(grads_body, grid=(count // rows,), in_specs=[block, whole(...]
    dynamic_slice x42 -> x0, local copies, waits for them, and re-layouts: 36.3 us -> none  [over_blocks(): carried, ignored = lax.scan(advance, carried, shaped)]
    all_to_all x1 -> x3, waiting for transfers between devices: 0.4 us -> 21.9 us  [the longest x1 13.1 us: body(): lax.all_to_all(dq.reshape(-1, tokens, width), QUERY_AXIS, 0, 0, tiled=True)]
    unnamed x45 -> x19, local copies, waits for them, and re-layouts: 21.2 us -> 5.54 us
  transfers between devices with their start and end apart: 7 -> 7, of which waited for: 5 -> 4; matrix products, arithmetic and copies ran while one was open for 20% -> 4% of each run, Pallas kernels for 0% -> 6%
where the time goes in v1:
time: 172 us; the launch traced here: 170 us
  blocking collectives  56 us (33%)
  Pallas kernels  40.1 us (23%)
  waiting for transfers between devices  32.8 us (19%)
  starting transfers between devices  29.9 us (17%)
  local copies, waits for them, and re-layouts  8.79 us (5%)
  other arithmetic  1.72 us (1%)
    all_to_all x1, blocking collectives, body(): lax.all_to_all(apart, (QUERY_AXIS, 'height'), 0, 0, tiled=True)  25.3 us
    pallas_call x1, Pallas kernels, local_grads(): pl.pallas_call(grads_body, grid=(count // rows,), in_specs=[block, whole(...  19.2 us
    all_to_all x1, blocking collectives, body(): lax.all_to_all(dkv.reshape(-1, tokens, 2 * width), KEY_AXES, 0, 0, tiled=...  15.9 us
    all_to_all x1, blocking collectives, body(): parts = lax.all_to_all(part, QUERY_AXIS, 0, 0, tiled=True)  14.8 us
    all_to_all x2, starting transfers between devices, spread_to(): return lax.all_to_all(copies, axes, 0, 0, tiled=True)  13.5 us
    all_to_all x1, waiting for transfers between devices, body(): lax.all_to_all(dq.reshape(-1, tokens, width), QUERY_AXIS, 0, 0, tiled=True)  13.1 us
    ppermute x2, waiting for transfers between devices, halo_pair(): high = lax.ppermute(lax.slice_in_dim(block, 0, 1, axis=dim), axis, backward)  10.9 us
    pallas_call x1, Pallas kernels, local_stats(): pl.pallas_call(lambda *refs: stats_body(*refs, rows=128), grid=(query_cou...  10.8 us
  transfers between devices with their start and end apart: 7, of which 4 were waited for; matrix products, arithmetic and copies ran while one was open for 4% of the time, Pallas kernels for 6%

profile of v1, /device:TPU:16, one launch (start us, length us, event | category | flops | bytes accessed | tf_op | source)
XLA Modules:
  0.0 170.0 jit_solution(16856359153876266057)
XLA Ops:
  0.6 0.0 copy-start.3
  0.6 0.0 copy-start.7
  0.7 0.9 pad_maximum_fusion
  1.6 1.0 broadcast_in_dim.4
  2.5 5.0 %all-to-all-start = ((bf16[8,224,256]{2,1,0:T(8,128)(2,1)}), bf16[8,224,256]{2,1,0:T(8,128)(2,1)S(1)}, u32[]{:S(2)}, u32[]{:S(2)}) async-start(bf16[8,224,256]{2,1,0:T(8,128)(2,1)} %broadcast_in_dim.4), calls=%async_computation | async-start | bytes 1835008 | tf_op jit(solution)/shard_map/all_to_all | solution.py:305
  7.6 0.0 copy-done.3
  7.6 0.0 copy-start.2
  7.6 0.7 fusion.1
  8.3 4.6 %collective-permute-start = (bf16[1,4,56,256]{3,2,1,0:T(8,128)(2,1)}, bf16[1,4,56,256]{3,2,1,0:T(8,128)(2,1)}, u32[]{:S(2)}, u32[]{:S(2)}) collective-permute-start(bf16[1,4,56,256]{3,2,1,0:T(8,128)(2,1)} %get-tuple-element.16), channel_id=1, source_target_pairs={{0,4},{4,8},{8,12},{12,16},{16,20},{20,24},{24,28},{28,32},{32,36}... | collective-permute-start | bytes 344072 | tf_op jit(solution)/shard_map/ppermute | solution.py:28
  12.9 8.8 %all-to-all-done = bf16[8,224,256]{2,1,0:T(8,128)(2,1)S(1)} async-done(((bf16[8,224,256]{2,1,0:T(8,128)(2,1)}), bf16[8,224,256]{2,1,0:T(8,128)(2,1)S(1)}, u32[]{:S(2)}, u32[]{:S(2)}) %all-to-all-start) | async-done | bytes 917536 | tf_op jit(solution)/shard_map/all_to_all | solution.py:305
  21.6 0.0 copy-done.7
  21.6 0.0 copy-start
  21.6 0.9 broadcast_in_dim.5
  22.5 8.5 %all-to-all-start.1 = ((bf16[8,224,128]{2,1,0:T(8,128)(2,1)}), bf16[8,224,128]{2,1,0:T(8,128)(2,1)S(1)}, u32[]{:S(2)}, u32[]{:S(2)}) async-start(bf16[8,224,128]{2,1,0:T(8,128)(2,1)} %broadcast_in_dim.5), calls=%async_computation.1 | async-start | bytes 917504 | tf_op jit(solution)/shard_map/all_to_all | solution.py:305
  31.0 1.3 collective-permute-start.1
  32.3 0.0 collective-permute-done.before_ref
  32.3 0.9 constant_dynamic-update-slice_fusion.2
  33.2 1.0 constant_dynamic-update-slice_fusion.1
  34.1 10.6 %collective-permute-done.1.after_ref = bf16[1,4,56,256]{3,2,1,0:T(8,128)(2,1)S(1)} collective-permute-done((bf16[1,4,56,256]{3,2,1,0:T(8,128)(2,1)}, bf16[1,4,56,256]{3,2,1,0:T(8,128)(2,1)S(1)}, u32[]{:S(2)}, u32[]{:S(2)}) %collective-permute-start.1) | collective-permute-done | bytes 114720 | tf_op jit(solution)/shard_map/ppermute | solution.py:29
  44.7 0.0 copy-start.4
  44.7 0.6 copy-done.4
  45.4 1.9 %collective-permute-start.2 = (bf16[4,1,56,256]{3,2,1,0:T(8,128)(2,1)S(1)}, bf16[4,1,56,256]{3,2,1,0:T(8,128)(2,1)S(1)}, u32[]{:S(2)}, u32[]{:S(2)}) collective-permute-start(bf16[4,1,56,256]{3,2,1,0:T(8,128)(2,1)S(1)} %get-tuple-element.14), channel_id=1, source_target_pairs={{0,1},{1,2},{2,3},{4,5},{5,6},{6,7},{8,9},{9,10},{10,11},{12,13},{... | collective-permute-start | bytes 344072 | tf_op jit(solution)/shard_map/ppermute | solution.py:28
  47.3 5.1 %collective-permute-start.3 = (bf16[4,1,56,256]{3,2,1,0:T(8,128)(2,1)S(1)}, bf16[4,1,56,256]{3,2,1,0:T(8,128)(2,1)S(1)}, u32[]{:S(2)}, u32[]{:S(2)}) collective-permute-start(bf16[4,1,56,256]{3,2,1,0:T(8,128)(2,1)S(1)} %get-tuple-element.13), channel_id=1, source_target_pairs={{1,0},{2,1},{3,2},{5,4},{6,5},{7,6},{9,8},{10,9},{11,10},{13,12},{... | collective-permute-start | bytes 344072 | tf_op jit(solution)/shard_map/ppermute | solution.py:29
  52.5 0.0 copy-done.2
  52.5 2.0 %copy.9 = bf16[64,8,8,256]{3,1,2,0:T(8,128)(2,1)} copy(bf16[64,8,8,256]{3,2,1,0:T(8,128)(2,1)S(1)} %bitcast.15) | data formatting | bytes 4194304
  54.5 0.0 copy-done
  54.5 0.0 collective-permute-done.2.above_ref
  54.5 0.0 copy-start.5
  54.5 0.3 collective-permute-done.3.below_ref
  54.8 0.3 copy-done.5
  55.2 0.0 copy-start.6
  55.2 0.6 copy-done.6
  55.8 10.1 %conv.1 = bf16[8,4,56,128]{3,2,1,0:T(8,128)(2,1)} custom-call(bf16[2,4,56,256]{3,2,1,0:T(8,128)(2,1)} %own_ref.1, bf16[1,4,56,256]{3,2,1,0:T(8,128)(2,1)} %collective-permute-done.before_ref, bf16[1,4,56,256]{3,2,1,0:T(8,128)(2,1)} %copy-done.4, bf16[4,1,56,256]{3,2,1,0:T(8,128)(2,1)} %copy-done.5, bf16[4,1,56,256]{3,2,1,0:T(8,128)(2,1)} %copy-done.6, ...), custom_call_target="tpu_custom_call" | custom-call | tf_op jit(solution)/shard_map/conv/pallas_call | solution.py:122
  65.9 0.0 all-to-all-done.1
  65.9 0.0 copy-start.1
  65.9 25.3 %all_to_all.30 = bf16[32,56,128]{2,1,0:T(8,128)(2,1)} all-to-all(bf16[32,56,128]{2,1,0:T(8,128)(2,1)} %bitcast.16), channel_id=1, replica_groups=mesh['x'=4,'y'=2,'z'=8,'height'=4] {'z','height'}, dimensions={0} | all-to-all | bytes 917504 | tf_op jit(solution)/shard_map/all_to_all | solution.py:323
  91.2 0.0 copy-done.1
  91.2 10.8 %stats.1 = (f32[8,4,1792]{2,1,0:T(4,128)}, bf16[128,1792]{1,0:T(8,128)(2,1)}, bf16[128,1792]{1,0:T(8,128)(2,1)}) custom-call(bf16[1792,256]{1,0:T(8,128)(2,1)} %bitcast.9, bf16[1792,128]{1,0:T(8,128)(2,1)} %bitcast.11, bf16[1792,128]{1,0:T(8,128)(2,1)} %bitcast.13), custom_call_target="tpu_custom_call" | custom-call | tf_op jit(solution)/shard_map/stats/pallas_call | solution.py:194
  102.0 14.8 %all_to_all.31.part_ref = f32[8,4,1792]{2,1,0:T(4,128)} all-to-all(f32[8,4,1792]{2,1,0:T(4,128)} %get-tuple-element.10), channel_id=1, replica_groups=mesh['x'=4,'y'=2,'z'=8,'height'=4] {'z'}, dimensions={0} | all-to-all | bytes 458752 | tf_op jit(solution)/shard_map/all_to_all | solution.py:325
  116.8 19.2 %grads.1 = (bf16[1792,256]{1,0:T(8,128)(2,1)}, bf16[1792,128]{1,0:T(8,128)(2,1)}) custom-call(bf16[1792,256]{1,0:T(8,128)(2,1)} %bitcast.10, bf16[1792,128]{1,0:T(8,128)(2,1)} %bitcast.12, bf16[1792,128]{1,0:T(8,128)(2,1)} %bitcast.14, bf16[128,1792]{1,0:T(8,128)(2,1)} %get-tuple-element.8.qt_ref, bf16[128,1792]{1,0:T(8,128)(2,1)} %get-tuple-element.9.gt_ref, ...), custom_call_target="tpu_custom_call" | custom-call | tf_op jit(solution)/shard_map/grads/pallas_call | solution.py:276
  136.0 15.9 %all_to_all.32 = bf16[8,224,256]{2,1,0:T(8,128)(2,1)S(1)} all-to-all(bf16[8,224,256]{2,1,0:T(8,128)(2,1)} %bitcast.17), channel_id=1, replica_groups=mesh['x'=4,'y'=2,'z'=8,'height'=4] {'x','y'}, dimensions={0} | all-to-all | bytes 1835008 | tf_op jit(solution)/shard_map/all_to_all | solution.py:327
  151.9 3.5 %all-to-all-start.4 = ((bf16[8,224,128]{2,1,0:T(8,128)(2,1)}), bf16[8,224,128]{2,1,0:T(8,128)(2,1)S(1)}, u32[]{:S(2)}, u32[]{:S(2)}) async-start(bf16[8,224,128]{2,1,0:T(8,128)(2,1)} %bitcast.18), calls=%async_computation.4 | async-start | bytes 917504 | tf_op jit(solution)/shard_map/all_to_all | solution.py:329
  155.4 0.1 reduce_sum.25
  155.6 0.6 fusion.2
  156.2 13.1 %all-to-all-done.4 = bf16[8,224,128]{2,1,0:T(8,128)(2,1)S(1)} async-done(((bf16[8,224,128]{2,1,0:T(8,128)(2,1)}), bf16[8,224,128]{2,1,0:T(8,128)(2,1)S(1)}, u32[]{:S(2)}, u32[]{:S(2)}) %all-to-all-start.4) | async-done | bytes 458784 | tf_op jit(solution)/shard_map/all_to_all | solution.py:329
  169.3 0.7 reduce_sum.24
  (2 shorter events, 0.0 us)
Async XLA Ops:
  0.6 6.9 %copy-start.3 = (bf16[2,4,56,256]{3,2,1,0:T(8,128)(2,1)S(1)}, bf16[2,4,56,256]{3,2,1,0:T(8,128)(2,1)}, u32[]{:S(2)}) copy-start(bf16[2,4,56,256]{3,2,1,0:T(8,128)(2,1)} %own_ref.1) | copy-start | bytes 688132
  0.6 21.0 %copy-start.7 = (bf16[224,128]{1,0:T(8,128)(2,1)S(1)}, bf16[224,128]{1,0:T(8,128)(2,1)}, u32[]{:S(2)}) copy-start(bf16[224,128]{1,0:T(8,128)(2,1)} %param.6) | copy-start | bytes 172036
  2.5 19.1 %all-to-all-start = ((bf16[8,224,256]{2,1,0:T(8,128)(2,1)}), bf16[8,224,256]{2,1,0:T(8,128)(2,1)S(1)}, u32[]{:S(2)}, u32[]{:S(2)}) async-start(bf16[8,224,256]{2,1,0:T(8,128)(2,1)} %broadcast_in_dim.4), calls=%async_computation | async-start | bytes 1835008 | tf_op jit(solution)/shard_map/all_to_all | solution.py:305
  7.6 44.9 %copy-start.2 = (bf16[512,8,256]{2,1,0:T(8,128)(2,1)S(1)}, bf16[512,8,256]{2,1,0:T(8,128)(2,1)}, u32[]{:S(2)}) copy-start(bf16[512,8,256]{2,1,0:T(8,128)(2,1)} %param.11) | copy-start | bytes 6291460
  8.3 24.0 %collective-permute-start = (bf16[1,4,56,256]{3,2,1,0:T(8,128)(2,1)}, bf16[1,4,56,256]{3,2,1,0:T(8,128)(2,1)}, u32[]{:S(2)}, u32[]{:S(2)}) collective-permute-start(bf16[1,4,56,256]{3,2,1,0:T(8,128)(2,1)} %get-tuple-element.16), channel_id=1, source_target_pairs={{0,4},{4,8},{8,12},{12,16},{16,20},{20,24},{24,28},{28,32},{32,36}... | collective-permute-start | bytes 344072 | tf_op jit(solution)/shard_map/ppermute | solution.py:28
  21.6 32.9 %copy-start = (bf16[8,224,256]{2,1,0:T(8,128)(2,1)}, bf16[8,224,256]{2,1,0:T(8,128)(2,1)S(1)}, u32[]{:S(2)}) copy-start(bf16[8,224,256]{2,1,0:T(8,128)(2,1)S(1)} %all-to-all-done) | copy-start | bytes 2752516
  22.5 43.4 %all-to-all-start.1 = ((bf16[8,224,128]{2,1,0:T(8,128)(2,1)}), bf16[8,224,128]{2,1,0:T(8,128)(2,1)S(1)}, u32[]{:S(2)}, u32[]{:S(2)}) async-start(bf16[8,224,128]{2,1,0:T(8,128)(2,1)} %broadcast_in_dim.5), calls=%async_computation.1 | async-start | bytes 917504 | tf_op jit(solution)/shard_map/all_to_all | solution.py:305
  31.0 13.7 %collective-permute-start.1 = (bf16[1,4,56,256]{3,2,1,0:T(8,128)(2,1)}, bf16[1,4,56,256]{3,2,1,0:T(8,128)(2,1)S(1)}, u32[]{:S(2)}, u32[]{:S(2)}) collective-permute-start(bf16[1,4,56,256]{3,2,1,0:T(8,128)(2,1)} %get-tuple-element.15), channel_id=1, source_target_pairs={{4,0},{8,4},{12,8},{16,12},{20,16},{24,20},{28,24},{32,28},{36,32}... | collective-permute-start | bytes 344072 | tf_op jit(solution)/shard_map/ppermute | solution.py:29
  44.7 0.6 copy-start.4
  45.4 9.1 %collective-permute-start.2 = (bf16[4,1,56,256]{3,2,1,0:T(8,128)(2,1)S(1)}, bf16[4,1,56,256]{3,2,1,0:T(8,128)(2,1)S(1)}, u32[]{:S(2)}, u32[]{:S(2)}) collective-permute-start(bf16[4,1,56,256]{3,2,1,0:T(8,128)(2,1)S(1)} %get-tuple-element.14), channel_id=1, source_target_pairs={{0,1},{1,2},{2,3},{4,5},{5,6},{6,7},{8,9},{9,10},{10,11},{12,13},{... | collective-permute-start | bytes 344072 | tf_op jit(solution)/shard_map/ppermute | solution.py:28
  47.3 7.5 %collective-permute-start.3 = (bf16[4,1,56,256]{3,2,1,0:T(8,128)(2,1)S(1)}, bf16[4,1,56,256]{3,2,1,0:T(8,128)(2,1)S(1)}, u32[]{:S(2)}, u32[]{:S(2)}) collective-permute-start(bf16[4,1,56,256]{3,2,1,0:T(8,128)(2,1)S(1)} %get-tuple-element.13), channel_id=1, source_target_pairs={{1,0},{2,1},{3,2},{5,4},{6,5},{7,6},{9,8},{10,9},{11,10},{13,12},{... | collective-permute-start | bytes 344072 | tf_op jit(solution)/shard_map/ppermute | solution.py:29
  54.5 0.7 copy-start.5
  55.2 0.6 copy-start.6
  65.9 25.3 %copy-start.1 = (bf16[8,224,128]{2,1,0:T(8,128)(2,1)}, bf16[8,224,128]{2,1,0:T(8,128)(2,1)S(1)}, u32[]{:S(2)}) copy-start(bf16[8,224,128]{2,1,0:T(8,128)(2,1)S(1)} %all-to-all-done.1) | copy-start | bytes 1376260
  151.9 17.4 %all-to-all-start.4 = ((bf16[8,224,128]{2,1,0:T(8,128)(2,1)}), bf16[8,224,128]{2,1,0:T(8,128)(2,1)S(1)}, u32[]{:S(2)}, u32[]{:S(2)}) async-start(bf16[8,224,128]{2,1,0:T(8,128)(2,1)} %bitcast.18), calls=%async_computation.4 | async-start | bytes 917504 | tf_op jit(solution)/shard_map/all_to_all | solution.py:329

commit v2 on v1

v2 whole, which is shorter than its diff:
```python
import math

import jax
import jax.numpy as jnp
from jax import lax
from jax.experimental import pallas as pl
from jax.experimental.pallas import tpu as pltpu
from jax.sharding import Mesh
from jax.sharding import PartitionSpec as P

HSZ = 64
LOSS_SCALE = 64.0
NEG_START = -1e30
HEAD_SCALE = 1.0 / math.sqrt(HSZ)
LOG2_SCALE = math.log2(math.e) / math.sqrt(HSZ)
KEY_AXES = ("x", "y")
QUERY_AXIS = "z"
DEPTH = ("x", "y", "z")
SPAN = 64
TILE = 256


def halo_pair(block, axis, dim):
    count = lax.axis_size(axis)
    forward = [(i, i + 1) for i in range(count - 1)]
    backward = [(target, source) for source, target in forward]
    last = lax.slice_in_dim(block, block.shape[dim] - 1, None, axis=dim)
    low = lax.ppermute(last, axis, forward)
    high = lax.ppermute(lax.slice_in_dim(block, 0, 1, axis=dim), axis, backward)
    return low, high


def product(left, right):
    return lax.dot_general(
        left, right, (((1,), (0,)), ((), ())), preferred_element_type=jnp.float32
    )


def product_t(left, right):
    return lax.dot_general(
        left, right, (((1,), (1,)), ((), ())), preferred_element_type=jnp.float32
    )


def conv_body(
    own_ref, before_ref, after_ref, above_ref, below_ref, w_ref, dec_ref, out_ref, x_ref, acc_ref, vox_ref, tok_ref
):
    planes, rows, cols, channels = own_ref.shape
    for d in range(planes + 2):
        for r in range(rows + 2):
            if r == 0:
                row = above_ref[d, 0]
            elif r == rows + 1:
                row = below_ref[d, 0]
            elif d == 0:
                row = before_ref[0, r - 1]
            elif d == planes + 1:
                row = after_ref[0, r - 1]
            else:
                row = own_ref[d - 1, r - 1]
            x_ref[d, r, :cols] = row
            x_ref[d, r, cols:] = jnp.zeros((SPAN - cols, channels), jnp.bfloat16)

    for step in range(9):
        along_depth, along_rows = (step // 3, step % 3)
        window = x_ref[2 - along_depth : 2 - along_depth + planes, 2 - along_rows : 2 - along_rows + rows]
        window = window.reshape(planes * rows * SPAN, channels)
        for tap in range(3):
            part = product_t(window, w_ref[along_depth, along_rows, tap])
            if step == 0:
                acc_ref[tap] = part
            else:
                acc_ref[tap] += part

    ahead = pltpu.roll(acc_ref[0], planes * rows * SPAN - 1, 0)
    summed = acc_ref[1] + ahead + pltpu.roll(acc_ref[2], 1, 0)
    voxels = (LOSS_SCALE * summed).astype(jnp.bfloat16).astype(jnp.float32)
    lanes = vox_ref.shape[2]
    for side in range(channels // lanes):
        vox_ref[side] = voxels[:, side * lanes : (side + 1) * lanes]
    half = SPAN // 2
    tokens = None
    for s in range(8):
        a, b, c = s // 4, s // 2 % 2, s % 2
        parts = []
        for h in range(rows // 2):
            at = pl.ds((a * rows + 2 * h + b) * SPAN + c, half, stride=2)
            sides = [vox_ref[side, at, :] for side in range(channels // lanes)]
            parts.append(jnp.concatenate(sides, axis=1))
        part = product_t(
            jnp.concatenate(parts, axis=0).astype(jnp.bfloat16),
            dec_ref[:, s * channels : (s + 1) * channels],
        )
        tokens = part if tokens is None else tokens + part
    for h in range(rows // 2):
        tok_ref[h * (cols // 2) : (h + 1) * (cols // 2), :] = tokens[
            h * half : h * half + cols // 2
        ]
    done = tok_ref[...].astype(jnp.bfloat16)
    copies, heights, _, width = out_ref.shape
    for place in range(copies):
        for height in range(heights):
            out_ref[place, height] = done[:, height * width : (height + 1) * width]


def conv_tokens(own, before, after, above, below, weight, decoder, copies, heights):
    planes, rows, cols, channels = own.shape
    tokens = planes // 2 * (rows // 2) * (cols // 2)
    features = decoder.shape[0]

    in_vmem = pl.BlockSpec(memory_space=pltpu.VMEM)
    out_shape = (copies, heights, tokens, features // heights)
    return pl.pallas_call(
        conv_body,
        in_specs=[in_vmem] * 7,
        out_specs=in_vmem,
        out_shape=jax.ShapeDtypeStruct(out_shape, jnp.bfloat16),
        scratch_shapes=[
            pltpu.VMEM((planes + 2, rows + 2, SPAN, channels), jnp.bfloat16),
            pltpu.VMEM((3, planes * rows * SPAN, channels), jnp.float32),
            pltpu.VMEM((channels // 128, planes * rows * SPAN, 128), jnp.float32),
            pltpu.VMEM((tokens, features), jnp.float32),
        ],
        name="conv",
    )(own, before, after, above, below, weight, decoder)


def own_rows(turned, head):
    rows = lax.broadcasted_iota(jnp.int32, turned.shape, 0) // HSZ
    return jnp.where(rows == head, turned, jnp.zeros_like(turned))


def stats_body(kv_ref, q_ref, g_ref, out_ref, qt_ref, gt_ref, *, rows):
    shards, _, per_shard, width = kv_ref.shape
    qt = q_ref[...].T
    gt = g_ref[...].T
    qt_ref[...] = qt
    gt_ref[...] = gt
    wide = qt.shape[1]
    for head in range(width // HSZ):
        qh = own_rows(qt, head)
        gh = own_rows(gt, head)

        zero = jnp.zeros((8, wide), jnp.float32)
        top, total, weighted = (jnp.full((8, wide), NEG_START, jnp.float32), zero, zero)
        for at in range(0, shards * per_shard, rows):
            span = pl.ds(at % per_shard, rows)
            logits = product(kv_ref[at // per_shard, 0, span], qh).reshape(rows // 8, 8, wide)
            slopes = product(kv_ref[at // per_shard, 1, span], gh).reshape(rows // 8, 8, wide)
            new_top = jnp.maximum(top, jnp.max(logits, axis=0))
            fade = jnp.exp2((top - new_top) * LOG2_SCALE)
            weights = jnp.exp2((logits - new_top[None]) * LOG2_SCALE)
            total = total * fade + jnp.sum(weights, axis=0)
            weighted = weighted * fade + jnp.sum(weights * slopes, axis=0)
            top = new_top
        best = jnp.max(top, axis=0, keepdims=True)
        fade = jnp.exp2((top - best) * LOG2_SCALE)
        total = jnp.sum(total * fade, axis=0, keepdims=True)
        weighted = jnp.sum(weighted * fade, axis=0, keepdims=True)
        log_sum = best * LOG2_SCALE + jnp.log2(total)
        delta = weighted / total
        for place in range(out_ref.shape[0]):
            out_ref[place, 2 * head : 2 * head + 1, :] = log_sum
            out_ref[place, 2 * head + 1 : 2 * head + 2, :] = delta


def local_stats(both, queries, grads, copies):
    query_count, width = queries.shape
    heads = width // HSZ
    tile = pl.BlockSpec((TILE, width), lambda i: (i, 0))
    turned = pl.BlockSpec((width, TILE), lambda i: (0, i))
    return pl.pallas_call(
        lambda *refs: stats_body(*refs, rows=112),
        grid=(query_count // TILE,),
        in_specs=[pl.BlockSpec(both.shape, lambda i: (0, 0, 0, 0)), tile, tile],
        out_specs=[
            pl.BlockSpec((copies, 2 * heads, TILE), lambda i: (0, 0, i)),
            turned,
            turned,
        ],
        out_shape=[
            jax.ShapeDtypeStruct((copies, 2 * heads, query_count), jnp.float32),
            jax.ShapeDtypeStruct((width, query_count), jnp.bfloat16),
            jax.ShapeDtypeStruct((width, query_count), jnp.bfloat16),
        ],
        name="stats",
    )(both, queries, grads)


def grads_body(kv_ref, q_ref, g_ref, qt_ref, gt_ref, part_ref, *rest):
    dkv_refs, (dq_ref, p_ref, s_ref, acc_ref, st_ref) = (rest[:-5], rest[-5:])
    block = pl.program_id(0)
    rows = kv_ref.shape[2]
    count, width = q_ref.shape

    @pl.when(block == 0)
    def _():
        for head in range(width // HSZ):
            logs = part_ref[:, 2 * head, :]
            best = jnp.max(logs, axis=0, keepdims=True)
            shares = jnp.exp2(logs - best)
            total = jnp.sum(shares, axis=0, keepdims=True)
            delta = jnp.sum(shares * part_ref[:, 2 * head + 1, :], axis=0, keepdims=True)
            st_ref[2 * head : 2 * head + 1, :] = best + jnp.log2(total)
            st_ref[2 * head + 1 : 2 * head + 2, :] = delta / total
        acc_ref[...] = jnp.zeros_like(acc_ref)

    keys = kv_ref[0, 0]
    values = kv_ref[0, 1]
    keys_t = keys.T
    head_of = lax.broadcasted_iota(jnp.int32, (rows, width), 1) // HSZ
    dks = []
    dvs = []
    for head in range(width // HSZ):
        mine = head_of == head
        head_keys = jnp.where(mine, keys, jnp.zeros_like(keys))
        head_values = jnp.where(mine, values, jnp.zeros_like(values))
        for i in range(count // TILE):
            at = slice(i * TILE, (i + 1) * TILE)
            logits = product(head_keys, qt_ref[:, at])
            slopes = product(head_values, gt_ref[:, at])
            probs = jnp.exp2(logits * LOG2_SCALE - st_ref[2 * head : 2 * head + 1, at])
            p_ref[head, :, at] = probs.astype(jnp.bfloat16)
            s_ref[head, :, at] = (probs * (slopes - st_ref[2 * head + 1 : 2 * head + 2, at])).astype(
                jnp.bfloat16
            )
        dvs.append(product(p_ref[head], g_ref[...]))
        dks.append(product(s_ref[head], q_ref[...]))
        span = slice(head * HSZ, (head + 1) * HSZ)
        acc_ref[span, :] += product(keys_t[span], s_ref[head])
    dk, dv = (dks[-1], dvs[-1])
    for head in range(len(dks) - 1):
        dk = jnp.where(head_of == head, dks[head], dk)
        dv = jnp.where(head_of == head, dvs[head], dv)
    dk = (dk * HEAD_SCALE).astype(jnp.bfloat16)
    dv = dv.astype(jnp.bfloat16)
    for shard, dkv_ref in enumerate(dkv_refs):

        @pl.when(block == shard)
        def _(dkv_ref=dkv_ref):
            dkv_ref[0] = dk
            dkv_ref[1] = dv

    @pl.when(block == pl.num_programs(0) - 1)
    def _():
        dq_ref[...] = (acc_ref[...] * HEAD_SCALE).T.astype(jnp.bfloat16)


def local_grads(both, queries, grads, queries_t, grads_t, parts):
    shards, _, rows, width = both.shape
    query_count = queries.shape[0]
    heads = width // HSZ

    def whole(*shape):
        return pl.BlockSpec(shape, lambda i: (0,) * len(shape))

    return pl.pallas_call(
        grads_body,
        grid=(shards,),
        in_specs=[
            pl.BlockSpec((1, 2, rows, width), lambda i: (i, 0, 0, 0)),
            whole(query_count, width),
            whole(query_count, width),
            whole(width, query_count),
            whole(width, query_count),
            whole(*parts.shape),
        ],
        out_specs=[whole(2, rows, width)] * shards + [whole(query_count, width)],
        out_shape=[jax.ShapeDtypeStruct((2, rows, width), jnp.bfloat16)] * shards
        + [jax.ShapeDtypeStruct((query_count, width), jnp.bfloat16)],
        scratch_shapes=[
            pltpu.VMEM((heads, rows, query_count), jnp.bfloat16),
            pltpu.VMEM((heads, rows, query_count), jnp.bfloat16),
            pltpu.VMEM((width, query_count), jnp.float32),
            pltpu.VMEM((2 * heads, query_count), jnp.float32),
        ],
        name="grads",
    )(both, queries, grads, queries_t, grads_t, parts)


def spread_to(array, axes):
    count = lax.axis_size(axes)
    copies = jnp.broadcast_to(array[None], (count,) + array.shape)
    return lax.all_to_all(copies, axes, 0, 0, tiled=True)


def moved(array, x_shift, y_shift):
    nx, ny = lax.axis_size("x"), lax.axis_size("y")
    pairs = [
        (x * ny + y, (x + x_shift) % nx * ny + (y + y_shift) % ny)
        for x in range(nx)
        for y in range(ny)
    ]
    return lax.ppermute(array, KEY_AXES, pairs)


X_SHIFTS = (0, 1, 3, 2)


def gathered_keys(own):
    other = moved(own, 0, 1)
    pair = jnp.stack([own, other])
    left = moved(pair, 1, 0)
    right = moved(pair, 3, 0)
    far = [moved(left[0], 1, 0), moved(right[1], 3, 0)]
    return jnp.concatenate([pair, left, right, jnp.stack(far)], axis=0)


def returned_keys(partial):
    total = partial[0].astype(jnp.float32)
    for at in range(1, len(partial)):
        total += moved(partial[at], -X_SHIFTS[at // 2], at % 2).astype(jnp.float32)
    return total.astype(jnp.bfloat16)


def body(queries, key_vectors, value_vectors, grad_conv, conv_weight, dec_weight):
    tokens, width = queries.shape
    heights = lax.axis_size("height")
    places = lax.axis_size(QUERY_AXIS)
    before, after = halo_pair(grad_conv, DEPTH, 0)
    padded = jnp.concatenate([before, grad_conv, after], axis=0)
    above, below = halo_pair(padded, "height", 1)
    both = gathered_keys(jnp.stack([key_vectors, value_vectors]))
    every_query = spread_to(queries, QUERY_AXIS).reshape(-1, width)
    decoder = dec_weight.reshape(dec_weight.shape[0], -1)
    apart = conv_tokens(
        grad_conv, before, after, above, below, conv_weight, decoder, places, heights
    )
    apart = apart.reshape((places * heights,) + apart.shape[2:])
    every_grad = lax.all_to_all(apart, (QUERY_AXIS, "height"), 0, 0, tiled=True)
    every_grad = every_grad.reshape(-1, width)
    part, queries_t, grads_t = local_stats(both, every_query, every_grad, places)
    parts = lax.all_to_all(part, QUERY_AXIS, 0, 0, tiled=True)
    *dkv, dq = local_grads(both, every_query, every_grad, queries_t, grads_t, parts)
    dq = lax.all_to_all(dq.reshape(-1, tokens, width), QUERY_AXIS, 0, 0, tiled=True)
    owned = returned_keys(dkv)
    dq = jnp.sum(dq.astype(jnp.float32), axis=0).astype(jnp.bfloat16)
    return dq, owned[0], owned[1]


def solution(mesh):
    fine = Mesh(mesh.devices.reshape(4, 2, 8, 4), ("x", "y", "z", "height"))
    in_specs = (
        P(DEPTH, "height"),
        P(DEPTH, "height"),
        P(DEPTH, "height"),
        P(DEPTH, "height", None, None),
        P(),
        P(),
    )
    out_specs = (P(DEPTH, "height"), P(DEPTH, "height"), P(DEPTH, "height"))
    return jax.shard_map(body, mesh=fine, in_specs=in_specs, out_specs=out_specs, check_vma=False)
```

time: 172 us -> 142 us (0.83)
  blocking collectives: 56 us -> 14.8 us
  starting transfers between devices: 29.9 us -> 55.2 us
  waiting for transfers between devices: 32.8 us -> 21.7 us
  local copies, waits for them, and re-layouts: 8.79 us -> 6.97 us
    all_to_all x2 -> x0, blocking collectives: 41.2 us -> none  [the longest x1 25.3 us: body(): lax.all_to_all(apart, (QUERY_AXIS, 'height'), 0, 0, tiled=True)]
    ppermute x0 -> x12, starting transfers between devices: none -> 18.7 us  [moved(): return lax.ppermute(array, KEY_AXES, pairs)]
    all_to_all x1, waiting for transfers between devices: 13.1 us -> 0.01 us  [body(): lax.all_to_all(dq.reshape(-1, tokens, width), QUERY_AXIS, 0, 0, tiled=True)]
    all_to_all x0 -> x1, waiting for transfers between devices: none -> 10.5 us  [body(): every_grad = lax.all_to_all(apart, (QUERY_AXIS, 'height'), 0, 0, tiled=True)]
    all_to_all x0 -> x1, starting transfers between devices: none -> 10.5 us  [body(): every_grad = lax.all_to_all(apart, (QUERY_AXIS, 'height'), 0, 0, tiled=True)]
    ppermute x2, waiting for transfers between devices: 10.9 us -> 1.81 us  [halo_pair(): high = lax.ppermute(lax.slice_in_dim(block, 0, 1, axis=dim), axis, backward)]
    ppermute x0 -> x12, waiting for transfers between devices: none -> 8.81 us  [moved(): return lax.ppermute(array, KEY_AXES, pairs)]
    all_to_all x2 -> x1, waiting for transfers between devices: 8.76 us -> 0.01 us  [spread_to(): return lax.all_to_all(copies, axes, 0, 0, tiled=True)]
  transfers between devices with their start and end apart: 7 -> 19, of which waited for: 4 -> 9; matrix products, arithmetic and copies ran while one was open for 4% -> 5% of each run, Pallas kernels for 6% -> 5%
where the time goes in v2:
time: 142 us; the launch traced here: 141 us
  starting transfers between devices  55.2 us (39%)
  Pallas kernels  38.4 us (27%)
  waiting for transfers between devices  21.7 us (15%)
  blocking collectives  14.8 us (10%)
  local copies, waits for them, and re-layouts  6.97 us (5%)
  other arithmetic  2.76 us (2%)
    pallas_call x1, Pallas kernels, local_grads(): pl.pallas_call(grads_body, grid=(shards,), in_specs=[pl.BlockSpec((1, 2,...  20.3 us
    ppermute x12, starting transfers between devices, moved(): return lax.ppermute(array, KEY_AXES, pairs)  18.7 us
    all_to_all x1, blocking collectives, body(): parts = lax.all_to_all(part, QUERY_AXIS, 0, 0, tiled=True)  14.8 us
    pallas_call x1, Pallas kernels, local_stats(): pl.pallas_call(lambda *refs: stats_body(*refs, rows=112), grid=(query_cou...  10.8 us
    all_to_all x1, waiting for transfers between devices, body(): every_grad = lax.all_to_all(apart, (QUERY_AXIS, 'height'), 0, 0, tiled=True)  10.5 us
    all_to_all x1, starting transfers between devices, body(): every_grad = lax.all_to_all(apart, (QUERY_AXIS, 'height'), 0, 0, tiled=True)  10.5 us
    all_to_all x1, starting transfers between devices, spread_to(): return lax.all_to_all(copies, axes, 0, 0, tiled=True)  10.4 us
    ppermute x12, waiting for transfers between devices, moved(): return lax.ppermute(array, KEY_AXES, pairs)  8.81 us
  transfers between devices with their start and end apart: 19, of which 9 were waited for; matrix products, arithmetic and copies ran while one was open for 5% of the time, Pallas kernels for 5%

profile of v2, /device:TPU:16, one launch (start us, length us, event | category | flops | bytes accessed | tf_op | source)
XLA Modules:
  0.0 140.8 jit_solution(2670251757624489923)
XLA Ops:
  0.6 1.0 fusion
  1.7 1.4 collective-permute-start
  3.0 1.0 fusion.2
  4.0 3.8 %collective-permute-start.5 = (bf16[1,4,56,256]{3,2,1,0:T(8,128)(2,1)S(1)}, bf16[1,4,56,256]{3,2,1,0:T(8,128)(2,1)S(1)}, u32[]{:S(2)}, u32[]{:S(2)}) collective-permute-start(bf16[1,4,56,256]{3,2,1,0:T(8,128)(2,1)S(1)} %get-tuple-element.30), channel_id=1, source_target_pairs={{0,4},{4,8},{8,12},{12,16},{16,20},{20,24},{24,28},{28,32},{32,36}... | collective-permute-start | bytes 344072 | tf_op jit(solution)/shard_map/ppermute | solution.py:28
  7.8 1.3 collective-permute-start.6
  9.1 1.7 %broadcast_in_dim.2 = bf16[8,224,128]{2,1,0:T(8,128)(2,1)} broadcast(bf16[224,128]{1,0:T(8,128)(2,1)} %param.6), dimensions={1,2} | broadcast | bytes 516096 | tf_op jit(solution)/shard_map/broadcast_in_dim | solution.py:283
  10.8 10.4 %all-to-all-start = ((bf16[8,224,128]{2,1,0:T(8,128)(2,1)}), bf16[8,224,128]{2,1,0:T(8,128)(2,1)S(1)}, u32[]{:S(2)}, u32[]{:S(2)}) async-start(bf16[8,224,128]{2,1,0:T(8,128)(2,1)} %broadcast_in_dim.2), calls=%async_computation | async-start | bytes 917504 | tf_op jit(solution)/shard_map/all_to_all | solution.py:284
  21.2 0.0 copy-start.7
  21.2 0.0 copy-start.8
  21.2 0.0 copy-start.4
  21.2 2.0 %copy.9 = bf16[64,8,8,256]{3,1,2,0:T(8,128)(2,1)} copy(bf16[64,8,8,256]{3,2,1,0:T(8,128)(2,1)S(1)} %bitcast.30) | data formatting | bytes 4194304
  23.3 0.0 collective-permute-done
  23.3 1.6 %collective-permute-start.1 = (bf16[2,2,224,128]{3,2,1,0:T(8,128)(2,1)S(1)}, bf16[2,2,224,128]{3,2,1,0:T(8,128)(2,1)S(1)}, u32[]{:S(2)}, u32[]{:S(2)}) collective-permute-start(bf16[2,2,224,128]{3,2,1,0:T(8,128)(2,1)S(1)} %pad_maximum_fusion), channel_id=1, source_target_pairs={{0,64},{32,96},{64,128},{96,160},{128,192},{160,224},{192,0},{224,... | collective-permute-start | bytes 688136 | tf_op jit(solution)/shard_map/ppermute | solution.py:294
  24.9 1.7 %collective-permute-start.2 = (bf16[2,2,224,128]{3,2,1,0:T(8,128)(2,1)S(1)}, bf16[2,2,224,128]{3,2,1,0:T(8,128)(2,1)S(1)}, u32[]{:S(2)}, u32[]{:S(2)}) collective-permute-start(bf16[2,2,224,128]{3,2,1,0:T(8,128)(2,1)S(1)} %pad_maximum_fusion), channel_id=1, source_target_pairs={{0,192},{32,224},{64,0},{96,32},{128,64},{160,96},{192,128},{224,1... | collective-permute-start | bytes 688136 | tf_op jit(solution)/shard_map/ppermute | solution.py:294
  26.8 1.9 %collective-permute-start.7 = (bf16[4,1,56,256]{3,2,1,0:T(8,128)(2,1)S(1)}, bf16[4,1,56,256]{3,2,1,0:T(8,128)(2,1)S(1)}, u32[]{:S(2)}, u32[]{:S(2)}) collective-permute-start(bf16[4,1,56,256]{3,2,1,0:T(8,128)(2,1)S(1)} %get-tuple-element.28), channel_id=1, source_target_pairs={{0,1},{1,2},{2,3},{4,5},{5,6},{6,7},{8,9},{9,10},{10,11},{12,13},{... | collective-permute-start | bytes 344072 | tf_op jit(solution)/shard_map/ppermute | solution.py:28
  28.7 5.1 %collective-permute-start.8 = (bf16[4,1,56,256]{3,2,1,0:T(8,128)(2,1)S(1)}, bf16[4,1,56,256]{3,2,1,0:T(8,128)(2,1)S(1)}, u32[]{:S(2)}, u32[]{:S(2)}) collective-permute-start(bf16[4,1,56,256]{3,2,1,0:T(8,128)(2,1)S(1)} %get-tuple-element.27), channel_id=1, source_target_pairs={{1,0},{2,1},{3,2},{5,4},{6,5},{7,6},{9,8},{10,9},{11,10},{13,12},{... | collective-permute-start | bytes 344072 | tf_op jit(solution)/shard_map/ppermute | solution.py:29
  33.9 0.5 collective-permute-done.7.above_ref
  34.4 1.8 %collective-permute-done.8.below_ref = bf16[4,1,56,256]{3,2,1,0:T(8,128)(2,1)S(1)} collective-permute-done((bf16[4,1,56,256]{3,2,1,0:T(8,128)(2,1)S(1)}, bf16[4,1,56,256]{3,2,1,0:T(8,128)(2,1)S(1)}, u32[]{:S(2)}, u32[]{:S(2)}) %collective-permute-start.8) | collective-permute-done | bytes 114720 | tf_op jit(solution)/shard_map/ppermute | solution.py:29
  36.2 0.6 copy-done.10
  36.8 7.4 %conv.1 = bf16[8,4,56,128]{3,2,1,0:T(8,128)(2,1)} custom-call(bf16[2,4,56,256]{3,2,1,0:T(8,128)(2,1)} %own_ref.1, bf16[1,4,56,256]{3,2,1,0:T(8,128)(2,1)} %copy-done.5, bf16[1,4,56,256]{3,2,1,0:T(8,128)(2,1)} %copy-done.6, bf16[4,1,56,256]{3,2,1,0:T(8,128)(2,1)} %copy-done.9, bf16[4,1,56,256]{3,2,1,0:T(8,128)(2,1)} %copy-done.10, ...), custom_call_target="tpu_custom_call" | custom-call | tf_op jit(solution)/shard_map/conv/pallas_call | solution.py:113
  44.2 0.4 collective-permute-start.3
  44.6 10.5 %all-to-all-start.1 = ((bf16[32,56,128]{2,1,0:T(8,128)(2,1)}), bf16[32,56,128]{2,1,0:T(8,128)(2,1)S(1)}, u32[]{:S(2)}, u32[]{:S(2)}) async-start(bf16[32,56,128]{2,1,0:T(8,128)(2,1)} %bitcast.31), calls=%async_computation.1 | async-start | bytes 917504 | tf_op jit(solution)/shard_map/all_to_all | solution.py:330
  55.1 0.0 collective-permute-done.2
  55.1 3.0 %collective-permute-start.4 = (bf16[2,224,128]{2,1,0:T(8,128)(2,1)S(1)}, bf16[2,224,128]{2,1,0:T(8,128)(2,1)S(1)}, u32[]{:S(2)}, u32[]{:S(2)}) collective-permute-start(bf16[2,224,128]{2,1,0:T(8,128)(2,1)S(1)} %slice_bitcast_fusion), channel_id=1, source_target_pairs={{0,192},{32,224},{64,0},{96,32},{128,64},{160,96},{192,128},{224,1... | collective-permute-start | bytes 344072 | tf_op jit(solution)/shard_map/ppermute | solution.py:294
  58.2 0.0 collective-permute-done.3
  58.2 2.6 %collective-permute-done.4 = bf16[2,224,128]{2,1,0:T(8,128)(2,1)S(1)} collective-permute-done((bf16[2,224,128]{2,1,0:T(8,128)(2,1)S(1)}, bf16[2,224,128]{2,1,0:T(8,128)(2,1)S(1)}, u32[]{:S(2)}, u32[]{:S(2)}) %collective-permute-start.4) | collective-permute-done | bytes 114720 | tf_op jit(solution)/shard_map/ppermute | solution.py:294
  60.8 10.5 %all-to-all-done.1 = bf16[32,56,128]{2,1,0:T(8,128)(2,1)S(1)} async-done(((bf16[32,56,128]{2,1,0:T(8,128)(2,1)}), bf16[32,56,128]{2,1,0:T(8,128)(2,1)S(1)}, u32[]{:S(2)}, u32[]{:S(2)}) %all-to-all-start.1) | async-done | bytes 458784 | tf_op jit(solution)/shard_map/all_to_all | solution.py:330
  71.3 0.8 copy-done.2
  72.1 10.8 %stats.1 = (f32[8,4,1792]{2,1,0:T(4,128)}, bf16[128,1792]{1,0:T(8,128)(2,1)}, bf16[128,1792]{1,0:T(8,128)(2,1)}) custom-call(bf16[8,2,224,128]{3,2,1,0:T(8,128)(2,1)} %copy-done, bf16[1792,128]{1,0:T(8,128)(2,1)} %bitcast.26, bf16[1792,128]{1,0:T(8,128)(2,1)} %bitcast.28), custom_call_target="tpu_custom_call" | custom-call | tf_op jit(solution)/shard_map/stats/pallas_call | solution.py:172
  82.9 14.8 %all_to_all.20.part_ref = f32[8,4,1792]{2,1,0:T(4,128)} all-to-all(f32[8,4,1792]{2,1,0:T(4,128)} %get-tuple-element.17), channel_id=1, replica_groups=mesh['x'=4,'y'=2,'z'=8,'height'=4] {'z'}, dimensions={0} | all-to-all | bytes 458752 | tf_op jit(solution)/shard_map/all_to_all | solution.py:333
  97.8 20.3 %grads.1 = (bf16[2,224,128]{2,1,0:T(8,128)(2,1)}, bf16[2,224,128]{2,1,0:T(8,128)(2,1)}, bf16[2,224,128]{2,1,0:T(8,128)(2,1)}, bf16[2,224,128]{2,1,0:T(8,128)(2,1...) custom-call(bf16[8,2,224,128]{3,2,1,0:T(8,128)(2,1)} %copy-done, ...), custom_call_target="tpu_custom_call" | custom-call | tf_op jit(solution)/shard_map/grads/pallas_call | solution.py:257
  118.0 3.5 %all-to-all-start.3 = ((bf16[8,224,128]{2,1,0:T(8,128)(2,1)}), bf16[8,224,128]{2,1,0:T(8,128)(2,1)S(1)}, u32[]{:S(2)}, u32[]{:S(2)}) async-start(bf16[8,224,128]{2,1,0:T(8,128)(2,1)} %bitcast.33), calls=%async_computation.3 | async-start | bytes 917504 | tf_op jit(solution)/shard_map/all_to_all | solution.py:335
  121.5 3.2 %collective-permute-start.10 = (bf16[2,224,128]{2,1,0:T(8,128)(2,1)}, bf16[2,224,128]{2,1,0:T(8,128)(2,1)S(1)}, u32[]{:S(2)}, u32[]{:S(2)}) collective-permute-start(bf16[2,224,128]{2,1,0:T(8,128)(2,1)} %get-tuple-element.21), channel_id=1, source_target_pairs={{0,192},{32,224},{64,0},{96,32},{128,64},{160,96},{192,128},{224,1... | collective-permute-start | bytes 344072 | tf_op jit(solution)/shard_map/ppermute | solution.py:294
  124.7 0.5 collective-permute-start.11
  125.2 1.7 %collective-permute-start.12 = (bf16[2,224,128]{2,1,0:T(8,128)(2,1)}, bf16[2,224,128]{2,1,0:T(8,128)(2,1)S(1)}, u32[]{:S(2)}, u32[]{:S(2)}) collective-permute-start(bf16[2,224,128]{2,1,0:T(8,128)(2,1)} %get-tuple-element.23), channel_id=1, source_target_pairs={{0,64},{32,96},{64,128},{96,160},{128,192},{160,224},{192,0},{224,... | collective-permute-start | bytes 344072 | tf_op jit(solution)/shard_map/ppermute | solution.py:294
  126.9 0.7 collective-permute-start.13
  127.6 3.0 %collective-permute-start.14 = (bf16[2,224,128]{2,1,0:T(8,128)(2,1)}, bf16[2,224,128]{2,1,0:T(8,128)(2,1)S(1)}, u32[]{:S(2)}, u32[]{:S(2)}) collective-permute-start(bf16[2,224,128]{2,1,0:T(8,128)(2,1)} %get-tuple-element.25), channel_id=1, source_target_pairs={{0,128},{32,160},{64,192},{96,224},{128,0},{160,32},{192,64},{224,... | collective-permute-start | bytes 344072 | tf_op jit(solution)/shard_map/ppermute | solution.py:294
  130.6 0.0 collective-permute-done.10
  130.6 0.7 collective-permute-start.15
  131.3 0.4 collective-permute-done.11
  131.7 0.9 collective-permute-start.9
  132.6 0.7 collective-permute-done.12
  133.3 3.3 %collective-permute-done.13 = bf16[2,224,128]{2,1,0:T(8,128)(2,1)S(1)} collective-permute-done((bf16[2,224,128]{2,1,0:T(8,128)(2,1)}, bf16[2,224,128]{2,1,0:T(8,128)(2,1)S(1)}, u32[]{:S(2)}, u32[]{:S(2)}) %collective-permute-start.13) | collective-permute-done | bytes 114720 | tf_op jit(solution)/shard_map/ppermute | solution.py:294
  136.6 1.4 %collective-permute-done.15 = bf16[2,224,128]{2,1,0:T(8,128)(2,1)S(1)} collective-permute-done((bf16[2,224,128]{2,1,0:T(8,128)(2,1)}, bf16[2,224,128]{2,1,0:T(8,128)(2,1)S(1)}, u32[]{:S(2)}, u32[]{:S(2)}) %collective-permute-start.15) | collective-permute-done | bytes 114720 | tf_op jit(solution)/shard_map/ppermute | solution.py:294
  138.0 0.4 collective-permute-done.9
  138.4 1.0 add_convert_fusion
  139.4 0.6 slice_bitcast_fusion.2
  140.1 0.7 reduce_sum.12
  (36 shorter events, 0.3 us)
Async XLA Ops:
  0.6 20.6 %copy-start.3 = (bf16[512,8,256]{2,1,0:T(8,128)(2,1)S(1)}, bf16[512,8,256]{2,1,0:T(8,128)(2,1)}, u32[]{:S(2)}) copy-start(bf16[512,8,256]{2,1,0:T(8,128)(2,1)} %param.11) | copy-start | bytes 6291460
  1.7 21.6 %collective-permute-start = (bf16[2,224,128]{2,1,0:T(8,128)(2,1)S(1)}, bf16[2,224,128]{2,1,0:T(8,128)(2,1)S(1)}, u32[]{:S(2)}, u32[]{:S(2)}) collective-permute-start(bf16[2,224,128]{2,1,0:T(8,128)(2,1)S(1)} %get-tuple-element.34), channel_id=1, source_target_pairs={{0,32},{32,0},{64,96},{96,64},{128,160},{160,128},{192,224},{224,1... | collective-permute-start | bytes 344072 | tf_op jit(solution)/shard_map/ppermute | solution.py:294
  4.0 22.7 %collective-permute-start.5 = (bf16[1,4,56,256]{3,2,1,0:T(8,128)(2,1)S(1)}, bf16[1,4,56,256]{3,2,1,0:T(8,128)(2,1)S(1)}, u32[]{:S(2)}, u32[]{:S(2)}) collective-permute-start(bf16[1,4,56,256]{3,2,1,0:T(8,128)(2,1)S(1)} %get-tuple-element.30), channel_id=1, source_target_pairs={{0,4},{4,8},{8,12},{12,16},{16,20},{20,24},{24,28},{28,32},{32,36}... | collective-permute-start | bytes 344072 | tf_op jit(solution)/shard_map/ppermute | solution.py:28
  7.8 18.9 %collective-permute-start.6 = (bf16[1,4,56,256]{3,2,1,0:T(8,128)(2,1)S(1)}, bf16[1,4,56,256]{3,2,1,0:T(8,128)(2,1)S(1)}, u32[]{:S(2)}, u32[]{:S(2)}) collective-permute-start(bf16[1,4,56,256]{3,2,1,0:T(8,128)(2,1)S(1)} %get-tuple-element.29), channel_id=1, source_target_pairs={{4,0},{8,4},{12,8},{16,12},{20,16},{24,20},{28,24},{32,28},{36,32}... | collective-permute-start | bytes 344072 | tf_op jit(solution)/shard_map/ppermute | solution.py:29
  10.8 33.8 %all-to-all-start = ((bf16[8,224,128]{2,1,0:T(8,128)(2,1)}), bf16[8,224,128]{2,1,0:T(8,128)(2,1)S(1)}, u32[]{:S(2)}, u32[]{:S(2)}) async-start(bf16[8,224,128]{2,1,0:T(8,128)(2,1)} %broadcast_in_dim.2), calls=%async_computation | async-start | bytes 917504 | tf_op jit(solution)/shard_map/all_to_all | solution.py:284
  21.2 2.1 %copy-start.7 = (bf16[224,128]{1,0:T(8,128)(2,1)S(1)}, bf16[224,128]{1,0:T(8,128)(2,1)}, u32[]{:S(2)}) copy-start(bf16[224,128]{1,0:T(8,128)(2,1)} %param.8) | copy-start | bytes 172036
  21.2 2.1 %copy-start.8 = (bf16[224,128]{1,0:T(8,128)(2,1)S(1)}, bf16[224,128]{1,0:T(8,128)(2,1)}, u32[]{:S(2)}) copy-start(bf16[224,128]{1,0:T(8,128)(2,1)} %param.7) | copy-start | bytes 172036
  21.2 5.4 %copy-start.4 = (bf16[2,4,56,256]{3,2,1,0:T(8,128)(2,1)S(1)}, bf16[2,4,56,256]{3,2,1,0:T(8,128)(2,1)}, u32[]{:S(2)}) copy-start(bf16[2,4,56,256]{3,2,1,0:T(8,128)(2,1)} %own_ref.1) | copy-start | bytes 688132
  23.3 20.9 %collective-permute-start.1 = (bf16[2,2,224,128]{3,2,1,0:T(8,128)(2,1)S(1)}, bf16[2,2,224,128]{3,2,1,0:T(8,128)(2,1)S(1)}, u32[]{:S(2)}, u32[]{:S(2)}) collective-permute-start(bf16[2,2,224,128]{3,2,1,0:T(8,128)(2,1)S(1)} %pad_maximum_fusion), channel_id=1, source_target_pairs={{0,64},{32,96},{64,128},{96,160},{128,192},{160,224},{192,0},{224,... | collective-permute-start | bytes 688136 | tf_op jit(solution)/shard_map/ppermute | solution.py:294
  24.9 30.2 %collective-permute-start.2 = (bf16[2,2,224,128]{3,2,1,0:T(8,128)(2,1)S(1)}, bf16[2,2,224,128]{3,2,1,0:T(8,128)(2,1)S(1)}, u32[]{:S(2)}, u32[]{:S(2)}) collective-permute-start(bf16[2,2,224,128]{3,2,1,0:T(8,128)(2,1)S(1)} %pad_maximum_fusion), channel_id=1, source_target_pairs={{0,192},{32,224},{64,0},{96,32},{128,64},{160,96},{192,128},{224,1... | collective-permute-start | bytes 688136 | tf_op jit(solution)/shard_map/ppermute | solution.py:294
  26.7 9.5 %copy-start.5 = (bf16[1,4,56,256]{3,2,1,0:T(8,128)(2,1)}, bf16[1,4,56,256]{3,2,1,0:T(8,128)(2,1)S(1)}, u32[]{:S(2)}) copy-start(bf16[1,4,56,256]{3,2,1,0:T(8,128)(2,1)S(1)} %collective-permute-done.5.before_ref) | copy-start | bytes 344068
  26.7 9.5 %copy-start.6 = (bf16[1,4,56,256]{3,2,1,0:T(8,128)(2,1)}, bf16[1,4,56,256]{3,2,1,0:T(8,128)(2,1)S(1)}, u32[]{:S(2)}) copy-start(bf16[1,4,56,256]{3,2,1,0:T(8,128)(2,1)S(1)} %collective-permute-done.6.after_ref) | copy-start | bytes 344068
  26.8 7.6 %collective-permute-start.7 = (bf16[4,1,56,256]{3,2,1,0:T(8,128)(2,1)S(1)}, bf16[4,1,56,256]{3,2,1,0:T(8,128)(2,1)S(1)}, u32[]{:S(2)}, u32[]{:S(2)}) collective-permute-start(bf16[4,1,56,256]{3,2,1,0:T(8,128)(2,1)S(1)} %get-tuple-element.28), channel_id=1, source_target_pairs={{0,1},{1,2},{2,3},{4,5},{5,6},{6,7},{8,9},{9,10},{10,11},{12,13},{... | collective-permute-start | bytes 344072 | tf_op jit(solution)/shard_map/ppermute | solution.py:28
  28.7 7.5 %collective-permute-start.8 = (bf16[4,1,56,256]{3,2,1,0:T(8,128)(2,1)S(1)}, bf16[4,1,56,256]{3,2,1,0:T(8,128)(2,1)S(1)}, u32[]{:S(2)}, u32[]{:S(2)}) collective-permute-start(bf16[4,1,56,256]{3,2,1,0:T(8,128)(2,1)S(1)} %get-tuple-element.27), channel_id=1, source_target_pairs={{1,0},{2,1},{3,2},{5,4},{6,5},{7,6},{9,8},{10,9},{11,10},{13,12},{... | collective-permute-start | bytes 344072 | tf_op jit(solution)/shard_map/ppermute | solution.py:29
  34.4 1.8 %copy-start.9 = (bf16[4,1,56,256]{3,2,1,0:T(8,128)(2,1)}, bf16[4,1,56,256]{3,2,1,0:T(8,128)(2,1)S(1)}, u32[]{:S(2)}) copy-start(bf16[4,1,56,256]{3,2,1,0:T(8,128)(2,1)S(1)} %collective-permute-done.7.above_ref) | copy-start | bytes 344068
  36.2 0.6 copy-start.10
  44.2 13.9 %collective-permute-start.3 = (bf16[2,224,128]{2,1,0:T(8,128)(2,1)S(1)}, bf16[2,224,128]{2,1,0:T(8,128)(2,1)S(1)}, u32[]{:S(2)}, u32[]{:S(2)}) collective-permute-start(bf16[2,224,128]{2,1,0:T(8,128)(2,1)S(1)} %slice_bitcast_fusion.1), channel_id=1, source_target_pairs={{0,64},{32,96},{64,128},{96,160},{128,192},{160,224},{192,0},{224,... | collective-permute-start | bytes 344072 | tf_op jit(solution)/shard_map/ppermute | solution.py:294
  44.6 26.7 %copy-start.1 = (bf16[8,224,128]{2,1,0:T(8,128)(2,1)}, bf16[8,224,128]{2,1,0:T(8,128)(2,1)S(1)}, u32[]{:S(2)}) copy-start(bf16[8,224,128]{2,1,0:T(8,128)(2,1)S(1)} %all-to-all-done) | copy-start | bytes 1376260
  44.6 26.7 %all-to-all-start.1 = ((bf16[32,56,128]{2,1,0:T(8,128)(2,1)}), bf16[32,56,128]{2,1,0:T(8,128)(2,1)S(1)}, u32[]{:S(2)}, u32[]{:S(2)}) async-start(bf16[32,56,128]{2,1,0:T(8,128)(2,1)} %bitcast.31), calls=%async_computation.1 | async-start | bytes 917504 | tf_op jit(solution)/shard_map/all_to_all | solution.py:330
  55.1 5.7 %collective-permute-start.4 = (bf16[2,224,128]{2,1,0:T(8,128)(2,1)S(1)}, bf16[2,224,128]{2,1,0:T(8,128)(2,1)S(1)}, u32[]{:S(2)}, u32[]{:S(2)}) collective-permute-start(bf16[2,224,128]{2,1,0:T(8,128)(2,1)S(1)} %slice_bitcast_fusion), channel_id=1, source_target_pairs={{0,192},{32,224},{64,0},{96,32},{128,64},{160,96},{192,128},{224,1... | collective-permute-start | bytes 344072 | tf_op jit(solution)/shard_map/ppermute | solution.py:294
  60.8 10.5 %copy-start = (bf16[8,2,224,128]{3,2,1,0:T(8,128)(2,1)}, bf16[8,2,224,128]{3,2,1,0:T(8,128)(2,1)S(1)}, u32[]{:S(2)}) copy-start(bf16[8,2,224,128]{3,2,1,0:T(8,128)(2,1)S(1)} %bitcast_dynamic-update-slice_fusion.refs_0_.kv_ref) | copy-start | bytes 2752516
  71.3 0.8 copy-start.2
  118.0 22.1 %all-to-all-start.3 = ((bf16[8,224,128]{2,1,0:T(8,128)(2,1)}), bf16[8,224,128]{2,1,0:T(8,128)(2,1)S(1)}, u32[]{:S(2)}, u32[]{:S(2)}) async-start(bf16[8,224,128]{2,1,0:T(8,128)(2,1)} %bitcast.33), calls=%async_computation.3 | async-start | bytes 917504 | tf_op jit(solution)/shard_map/all_to_all | solution.py:335
  121.5 9.1 %collective-permute-start.10 = (bf16[2,224,128]{2,1,0:T(8,128)(2,1)}, bf16[2,224,128]{2,1,0:T(8,128)(2,1)S(1)}, u32[]{:S(2)}, u32[]{:S(2)}) collective-permute-start(bf16[2,224,128]{2,1,0:T(8,128)(2,1)} %get-tuple-element.21), channel_id=1, source_target_pairs={{0,192},{32,224},{64,0},{96,32},{128,64},{160,96},{192,128},{224,1... | collective-permute-start | bytes 344072 | tf_op jit(solution)/shard_map/ppermute | solution.py:294
  124.7 7.1 %collective-permute-start.11 = (bf16[2,224,128]{2,1,0:T(8,128)(2,1)}, bf16[2,224,128]{2,1,0:T(8,128)(2,1)S(1)}, u32[]{:S(2)}, u32[]{:S(2)}) collective-permute-start(bf16[2,224,128]{2,1,0:T(8,128)(2,1)} %get-tuple-element.22), channel_id=1, source_target_pairs={{0,224},{32,192},{64,32},{96,0},{128,96},{160,64},{192,160},{224,1... | collective-permute-start | bytes 344072 | tf_op jit(solution)/shard_map/ppermute | solution.py:294
  125.2 8.1 %collective-permute-start.12 = (bf16[2,224,128]{2,1,0:T(8,128)(2,1)}, bf16[2,224,128]{2,1,0:T(8,128)(2,1)S(1)}, u32[]{:S(2)}, u32[]{:S(2)}) collective-permute-start(bf16[2,224,128]{2,1,0:T(8,128)(2,1)} %get-tuple-element.23), channel_id=1, source_target_pairs={{0,64},{32,96},{64,128},{96,160},{128,192},{160,224},{192,0},{224,... | collective-permute-start | bytes 344072 | tf_op jit(solution)/shard_map/ppermute | solution.py:294
  126.9 9.7 %collective-permute-start.13 = (bf16[2,224,128]{2,1,0:T(8,128)(2,1)}, bf16[2,224,128]{2,1,0:T(8,128)(2,1)S(1)}, u32[]{:S(2)}, u32[]{:S(2)}) collective-permute-start(bf16[2,224,128]{2,1,0:T(8,128)(2,1)} %get-tuple-element.24), channel_id=1, source_target_pairs={{0,96},{32,64},{64,160},{96,128},{128,224},{160,192},{192,32},{224... | collective-permute-start | bytes 344072 | tf_op jit(solution)/shard_map/ppermute | solution.py:294
  127.6 9.0 %collective-permute-start.14 = (bf16[2,224,128]{2,1,0:T(8,128)(2,1)}, bf16[2,224,128]{2,1,0:T(8,128)(2,1)S(1)}, u32[]{:S(2)}, u32[]{:S(2)}) collective-permute-start(bf16[2,224,128]{2,1,0:T(8,128)(2,1)} %get-tuple-element.25), channel_id=1, source_target_pairs={{0,128},{32,160},{64,192},{96,224},{128,0},{160,32},{192,64},{224,... | collective-permute-start | bytes 344072 | tf_op jit(solution)/shard_map/ppermute | solution.py:294
  130.6 7.4 %collective-permute-start.15 = (bf16[2,224,128]{2,1,0:T(8,128)(2,1)}, bf16[2,224,128]{2,1,0:T(8,128)(2,1)S(1)}, u32[]{:S(2)}, u32[]{:S(2)}) collective-permute-start(bf16[2,224,128]{2,1,0:T(8,128)(2,1)} %get-tuple-element.26), channel_id=1, source_target_pairs={{0,160},{32,128},{64,224},{96,192},{128,32},{160,0},{192,96},{224,... | collective-permute-start | bytes 344072 | tf_op jit(solution)/shard_map/ppermute | solution.py:294
  131.7 6.7 %collective-permute-start.9 = (bf16[2,224,128]{2,1,0:T(8,128)(2,1)}, bf16[2,224,128]{2,1,0:T(8,128)(2,1)S(1)}, u32[]{:S(2)}, u32[]{:S(2)}) collective-permute-start(bf16[2,224,128]{2,1,0:T(8,128)(2,1)} %get-tuple-element.20), channel_id=1, source_target_pairs={{0,32},{32,0},{64,96},{96,64},{128,160},{160,128},{192,224},{224,1... | collective-permute-start | bytes 344072 | tf_op jit(solution)/shard_map/ppermute | solution.py:294

commit v3 on v2

--- a/solution.py
+++ b/solution.py
@@ -18,6 +18,7 @@
 DEPTH = ("x", "y", "z")
 SPAN = 64
 TILE = 256
+GROUP = 2
 
 
 def halo_pair(block, axis, dim):
@@ -130,9 +131,19 @@
     return jnp.where(rows == head, turned, jnp.zeros_like(turned))
 
 
-def stats_body(kv_ref, q_ref, g_ref, out_ref, qt_ref, gt_ref, *, rows):
+def stats_body(kv_ref, place_ref, g_ref, *refs, rows):
+    q_refs, (out_ref, q_ref, qt_ref, gt_ref) = (refs[:-4], refs[-4:])
     shards, _, per_shard, width = kv_ref.shape
-    qt = q_ref[...].T
+
+    @pl.when(pl.program_id(0) == 0)
+    def _():
+        count = len(q_refs)
+        for back, shard_ref in enumerate(q_refs):
+            at = (place_ref[0] + (count - back)) % count
+            tokens = shard_ref.shape[0]
+            q_ref[pl.ds(pl.multiple_of(at * tokens, tokens), tokens), :] = shard_ref[...]
+
+    qt = q_ref[pl.ds(pl.multiple_of(pl.program_id(0) * TILE, TILE), TILE), :].T
     gt = g_ref[...].T
     qt_ref[...] = qt
     gt_ref[...] = gt
@@ -164,33 +175,42 @@
             out_ref[place, 2 * head + 1 : 2 * head + 2, :] = delta
 
 
-def local_stats(both, queries, grads, copies):
-    query_count, width = queries.shape
+def local_stats(both, shards, grads, copies):
+    query_count, width = grads.shape
+    place = lax.axis_index(QUERY_AXIS).astype(jnp.int32).reshape(1)
     heads = width // HSZ
     tile = pl.BlockSpec((TILE, width), lambda i: (i, 0))
     turned = pl.BlockSpec((width, TILE), lambda i: (0, i))
     return pl.pallas_call(
         lambda *refs: stats_body(*refs, rows=112),
         grid=(query_count // TILE,),
-        in_specs=[pl.BlockSpec(both.shape, lambda i: (0, 0, 0, 0)), tile, tile],
+        in_specs=[
+            pl.BlockSpec(both.shape, lambda i: (0, 0, 0, 0)),
+            pl.BlockSpec(memory_space=pltpu.SMEM),
+            tile,
+        ]
+        + [pl.BlockSpec(shards[0].shape, lambda i: (0, 0))] * len(shards),
         out_specs=[
             pl.BlockSpec((copies, 2 * heads, TILE), lambda i: (0, 0, i)),
+            pl.BlockSpec((query_count, width), lambda i: (0, 0)),
             turned,
             turned,
         ],
         out_shape=[
             jax.ShapeDtypeStruct((copies, 2 * heads, query_count), jnp.float32),
+            jax.ShapeDtypeStruct((query_count, width), jnp.bfloat16),
             jax.ShapeDtypeStruct((width, query_count), jnp.bfloat16),
             jax.ShapeDtypeStruct((width, query_count), jnp.bfloat16),
         ],
         name="stats",
-    )(both, queries, grads)
+    )(both, place, grads, *shards)
 
 
 def grads_body(kv_ref, q_ref, g_ref, qt_ref, gt_ref, part_ref, *rest):
     dkv_refs, (dq_ref, p_ref, s_ref, acc_ref, st_ref) = (rest[:-5], rest[-5:])
     block = pl.program_id(0)
-    rows = kv_ref.shape[2]
+    group, _, per_shard, _ = kv_ref.shape
+    rows = group * per_shard
     count, width = q_ref.shape
 
     @pl.when(block == 0)
@@ -205,8 +225,8 @@
             st_ref[2 * head + 1 : 2 * head + 2, :] = delta / total
         acc_ref[...] = jnp.zeros_like(acc_ref)
 
-    keys = kv_ref[0, 0]
-    values = kv_ref[0, 1]
+    keys = kv_ref[:, 0].reshape(rows, width)
+    values = kv_ref[:, 1].reshape(rows, width)
     keys_t = keys.T
     head_of = lax.broadcasted_iota(jnp.int32, (rows, width), 1) // HSZ
     dks = []
@@ -236,10 +256,12 @@
     dv = dv.astype(jnp.bfloat16)
     for shard, dkv_ref in enumerate(dkv_refs):
 
-        @pl.when(block == shard)
-        def _(dkv_ref=dkv_ref):
-            dkv_ref[0] = dk
-            dkv_ref[1] = dv
+        span = slice(shard % group * per_shard, (shard % group + 1) * per_shard)
+
+        @pl.when(block == shard // group)
+        def _(dkv_ref=dkv_ref, span=span):
+            dkv_ref[0] = dk[span]
+            dkv_ref[1] = dv[span]
 
     @pl.when(block == pl.num_programs(0) - 1)
     def _():
@@ -256,9 +278,9 @@
 
     return pl.pallas_call(
         grads_body,
-        grid=(shards,),
+        grid=(shards // GROUP,),
         in_specs=[
-            pl.BlockSpec((1, 2, rows, width), lambda i: (i, 0, 0, 0)),
+            pl.BlockSpec((GROUP, 2, rows, width), lambda i: (i, 0, 0, 0)),
             whole(query_count, width),
             whole(query_count, width),
             whole(width, query_count),
@@ -269,8 +291,8 @@
         out_shape=[jax.ShapeDtypeStruct((2, rows, width), jnp.bfloat16)] * shards
         + [jax.ShapeDtypeStruct((query_count, width), jnp.bfloat16)],
         scratch_shapes=[
-            pltpu.VMEM((heads, rows, query_count), jnp.bfloat16),
-            pltpu.VMEM((heads, rows, query_count), jnp.bfloat16),
+            pltpu.VMEM((heads, GROUP * rows, query_count), jnp.bfloat16),
+            pltpu.VMEM((heads, GROUP * rows, query_count), jnp.bfloat16),
             pltpu.VMEM((width, query_count), jnp.float32),
             pltpu.VMEM((2 * heads, query_count), jnp.float32),
         ],
@@ -278,10 +300,19 @@
     )(both, queries, grads, queries_t, grads_t, parts)
 
 
-def spread_to(array, axes):
-    count = lax.axis_size(axes)
-    copies = jnp.broadcast_to(array[None], (count,) + array.shape)
-    return lax.all_to_all(copies, axes, 0, 0, tiled=True)
+def ring_step(array, shift):
+    count = lax.axis_size(QUERY_AXIS)
+    return lax.ppermute(array, QUERY_AXIS, [(i, (i + shift) % count) for i in range(count)])
+
+
+def gathered_queries(own):
+    up, down = [ring_step(own, 1)], [ring_step(own, -1)]
+    up.append(ring_step(up[-1], 1))
+    down.append(ring_step(down[-1], -1))
+    up.append(ring_step(up[-1], 1))
+    down.append(ring_step(down[-1], -1))
+    up.append(ring_step(up[-1], 1))
+    return [own] + up + down[::-1]
 
 
 def moved(array, x_shift, y_shift):
@@ -321,7 +352,7 @@
     padded = jnp.concatenate([before, grad_conv, after], axis=0)
     above, below = halo_pair(padded, "height", 1)
     both = gathered_keys(jnp.stack([key_vectors, value_vectors]))
-    every_query = spread_to(queries, QUERY_AXIS).reshape(-1, width)
+    query_shards = gathered_queries(queries)
     decoder = dec_weight.reshape(dec_weight.shape[0], -1)
     apart = conv_tokens(
         grad_conv, before, after, above, below, conv_weight, decoder, places, heights
@@ -329,7 +360,7 @@
     apart = apart.reshape((places * heights,) + apart.shape[2:])
     every_grad = lax.all_to_all(apart, (QUERY_AXIS, "height"), 0, 0, tiled=True)
     every_grad = every_grad.reshape(-1, width)
-    part, queries_t, grads_t = local_stats(both, every_query, every_grad, places)
+    part, every_query, queries_t, grads_t = local_stats(both, query_shards, every_grad, places)
     parts = lax.all_to_all(part, QUERY_AXIS, 0, 0, tiled=True)
     *dkv, dq = local_grads(both, every_query, every_grad, queries_t, grads_t, parts)
     dq = lax.all_to_all(dq.reshape(-1, tokens, width), QUERY_AXIS, 0, 0, tiled=True)

time: 142 us -> 140 us (0.986)
  starting transfers between devices: 55.2 us -> 50.6 us
  waiting for transfers between devices: 21.7 us -> 24.1 us
    ppermute x0 -> x7, starting transfers between devices: none -> 12.3 us  [ring_step(): lax.ppermute(array, QUERY_AXIS, [(i, (i + shift) % count) for i in range(...]
    all_to_all x1 -> x0, starting transfers between devices: 10.4 us -> none  [spread_to(): return lax.all_to_all(copies, axes, 0, 0, tiled=True)]
    ppermute x0 -> x7, waiting for transfers between devices: none -> 5.25 us  [ring_step(): lax.ppermute(array, QUERY_AXIS, [(i, (i + shift) % count) for i in range(...]
    ppermute x2, starting transfers between devices: 6.44 us -> 3.21 us  [halo_pair(): high = lax.ppermute(lax.slice_in_dim(block, 0, 1, axis=dim), axis, backward)]
    all_to_all x1, starting transfers between devices: 10.5 us -> 7.98 us  [body(): every_grad = lax.all_to_all(apart, (QUERY_AXIS, 'height'), 0, 0, tiled=True)]
    ppermute x12, starting transfers between devices: 18.7 us -> 16.7 us  [moved(): return lax.ppermute(array, KEY_AXES, pairs)]
    ppermute x2, waiting for transfers between devices: 1.81 us -> 0.01 us  [halo_pair(): high = lax.ppermute(lax.slice_in_dim(block, 0, 1, axis=dim), axis, backward)]
    all_to_all x1, waiting for transfers between devices: 10.5 us -> 8.85 us  [body(): every_grad = lax.all_to_all(apart, (QUERY_AXIS, 'height'), 0, 0, tiled=True)]
  transfers between devices with their start and end apart: 19 -> 25, of which waited for: 9 -> 5; matrix products, arithmetic and copies ran while one was open for 5% -> 6% of each run, Pallas kernels for 5% -> 5%
where the time goes in v3:
time: 140 us; the launch traced here: 139 us
  starting transfers between devices  50.6 us (36%)
  Pallas kernels  37.7 us (27%)
  waiting for transfers between devices  24.1 us (17%)
  blocking collectives  14.8 us (11%)
  local copies, waits for them, and re-layouts  6.89 us (5%)
  other arithmetic  3.46 us (2%)
    pallas_call x1, Pallas kernels, local_grads(): pl.pallas_call(grads_body, grid=(shards // GROUP,), in_specs=[pl.BlockSpe...  19.2 us
    ppermute x12, starting transfers between devices, moved(): return lax.ppermute(array, KEY_AXES, pairs)  16.7 us
    all_to_all x1, blocking collectives, body(): parts = lax.all_to_all(part, QUERY_AXIS, 0, 0, tiled=True)  14.8 us
    ppermute x7, starting transfers between devices, ring_step(): lax.ppermute(array, QUERY_AXIS, [(i, (i + shift) % count) for i in range(...  12.3 us
    pallas_call x1, Pallas kernels, local_stats(): pl.pallas_call(lambda *refs: stats_body(*refs, rows=112), grid=(query_cou...  11.1 us
    ppermute x12, waiting for transfers between devices, moved(): return lax.ppermute(array, KEY_AXES, pairs)  10 us
    all_to_all x1, waiting for transfers between devices, body(): every_grad = lax.all_to_all(apart, (QUERY_AXIS, 'height'), 0, 0, tiled=True)  8.85 us
    all_to_all x1, starting transfers between devices, body(): every_grad = lax.all_to_all(apart, (QUERY_AXIS, 'height'), 0, 0, tiled=True)  7.98 us
  transfers between devices with their start and end apart: 25, of which 5 were waited for; matrix products, arithmetic and copies ran while one was open for 6% of the time, Pallas kernels for 5%

profile of v3, /device:TPU:16, one launch (start us, length us, event | category | flops | bytes accessed | tf_op | source)
XLA Modules:
  0.0 138.5 jit_solution(13679309907684917375)
XLA Ops:
  0.6 2.0 %collective-permute-start.9 = (bf16[224,128]{1,0:T(8,128)(2,1)}, bf16[224,128]{1,0:T(8,128)(2,1)S(1)}, u32[]{:S(2)}, u32[]{:S(2)}) collective-permute-start(bf16[224,128]{1,0:T(8,128)(2,1)} %refs_3_.1), channel_id=1, source_target_pairs={{0,4},{4,8},{8,12},{12,16},{16,20},{20,24},{24,28},{28,0},{1,5},{5... | collective-permute-start | bytes 172040 | tf_op jit(solution)/shard_map/ppermute | solution.py:305
  2.6 4.0 %collective-permute-start.13 = (bf16[224,128]{1,0:T(8,128)(2,1)}, bf16[224,128]{1,0:T(8,128)(2,1)S(1)}, u32[]{:S(2)}, u32[]{:S(2)}) collective-permute-start(bf16[224,128]{1,0:T(8,128)(2,1)} %refs_3_.1), channel_id=1, source_target_pairs={{0,28},{4,0},{8,4},{12,8},{16,12},{20,16},{24,20},{28,24},{1,29},{... | collective-permute-start | bytes 172040 | tf_op jit(solution)/shard_map/ppermute | solution.py:305
  6.7 0.9 fusion
  7.5 1.4 collective-permute-start
  8.9 1.0 fusion.2
  9.9 1.3 collective-permute-start.6
  11.2 4.6 %collective-permute-start.5 = (bf16[1,4,56,256]{3,2,1,0:T(8,128)(2,1)S(1)}, bf16[1,4,56,256]{3,2,1,0:T(8,128)(2,1)S(1)}, u32[]{:S(2)}, u32[]{:S(2)}) collective-permute-start(bf16[1,4,56,256]{3,2,1,0:T(8,128)(2,1)S(1)} %get-tuple-element.32), channel_id=1, source_target_pairs={{0,4},{4,8},{8,12},{12,16},{16,20},{20,24},{24,28},{28,32},{32,36}... | collective-permute-start | bytes 344072 | tf_op jit(solution)/shard_map/ppermute | solution.py:29
  15.7 0.9 constant_dynamic-update-slice_fusion.3
  16.6 3.7 %copy.9 = bf16[64,8,8,256]{3,1,2,0:T(8,128)(2,1)} copy(bf16[64,8,8,256]{3,2,1,0:T(8,128)(2,1)} %bitcast.28) | data formatting | bytes 4194304
  20.3 0.0 collective-permute-done.9.refs_4_
  20.3 0.0 collective-permute-start.10
  20.3 0.0 collective-permute-done.13.refs_10_
  20.3 4.1 %collective-permute-start.14 = (bf16[224,128]{1,0:T(8,128)(2,1)S(1)}, bf16[224,128]{1,0:T(8,128)(2,1)S(1)}, u32[]{:S(2)}, u32[]{:S(2)}) collective-permute-start(bf16[224,128]{1,0:T(8,128)(2,1)S(1)} %collective-permute-done.13.refs_10_), channel_id=1, source_target_pairs={{0,28},{4,0},{8,4},{12,8},{16,12},{20,16},{24,20},{28,24},{1,29},{... | collective-permute-start | bytes 172040 | tf_op jit(solution)/shard_map/ppermute | solution.py:305
  24.4 0.0 collective-permute-done
  24.4 2.8 %collective-permute-start.2 = (bf16[2,2,224,128]{3,2,1,0:T(8,128)(2,1)S(1)}, bf16[2,2,224,128]{3,2,1,0:T(8,128)(2,1)S(1)}, u32[]{:S(2)}, u32[]{:S(2)}) collective-permute-start(bf16[2,2,224,128]{3,2,1,0:T(8,128)(2,1)S(1)} %pad_maximum_fusion), channel_id=1, source_target_pairs={{0,192},{32,224},{64,0},{96,32},{128,64},{160,96},{192,128},{224,1... | collective-permute-start | bytes 688136 | tf_op jit(solution)/shard_map/ppermute | solution.py:325
  27.4 1.9 %collective-permute-start.8 = (bf16[4,1,56,256]{3,2,1,0:T(8,128)(2,1)S(1)}, bf16[4,1,56,256]{3,2,1,0:T(8,128)(2,1)S(1)}, u32[]{:S(2)}, u32[]{:S(2)}) collective-permute-start(bf16[4,1,56,256]{3,2,1,0:T(8,128)(2,1)S(1)} %get-tuple-element.29), channel_id=1, source_target_pairs={{1,0},{2,1},{3,2},{5,4},{6,5},{7,6},{9,8},{10,9},{11,10},{13,12},{... | collective-permute-start | bytes 344072 | tf_op jit(solution)/shard_map/ppermute | solution.py:30
  29.3 2.4 %collective-permute-start.7 = (bf16[4,1,56,256]{3,2,1,0:T(8,128)(2,1)S(1)}, bf16[4,1,56,256]{3,2,1,0:T(8,128)(2,1)S(1)}, u32[]{:S(2)}, u32[]{:S(2)}) collective-permute-start(bf16[4,1,56,256]{3,2,1,0:T(8,128)(2,1)S(1)} %get-tuple-element.30), channel_id=1, source_target_pairs={{0,1},{1,2},{2,3},{4,5},{5,6},{6,7},{8,9},{9,10},{10,11},{12,13},{... | collective-permute-start | bytes 344072 | tf_op jit(solution)/shard_map/ppermute | solution.py:29
  31.8 0.0 copy-start.9
  31.8 0.1 collective-permute-start.11
  31.9 0.0 collective-permute-done.14.refs_9_
  31.9 0.1 collective-permute-start.1
  32.0 5.2 %collective-permute-done.11.refs_6_ = bf16[224,128]{1,0:T(8,128)(2,1)S(1)} collective-permute-done((bf16[224,128]{1,0:T(8,128)(2,1)S(1)}, bf16[224,128]{1,0:T(8,128)(2,1)S(1)}, u32[]{:S(2)}, u32[]{:S(2)}) %collective-permute-start.11) | collective-permute-done | bytes 57376 | tf_op jit(solution)/shard_map/ppermute | solution.py:305
  37.2 0.7 collective-permute-start.15
  38.0 1.3 collective-permute-start.12
  39.3 0.6 copy-done.6
  39.9 7.4 %conv.1 = bf16[8,4,56,128]{3,2,1,0:T(8,128)(2,1)} custom-call(bf16[2,4,56,256]{3,2,1,0:T(8,128)(2,1)} %own_ref.1, bf16[1,4,56,256]{3,2,1,0:T(8,128)(2,1)} %copy-done.4, bf16[1,4,56,256]{3,2,1,0:T(8,128)(2,1)} %copy-done.3, bf16[4,1,56,256]{3,2,1,0:T(8,128)(2,1)} %copy-done.6, bf16[4,1,56,256]{3,2,1,0:T(8,128)(2,1)} %copy-done.5, ...), custom_call_target="tpu_custom_call" | custom-call | tf_op jit(solution)/shard_map/conv/pallas_call | solution.py:114
  47.3 8.0 %all-to-all-start = ((bf16[32,56,128]{2,1,0:T(8,128)(2,1)}), bf16[32,56,128]{2,1,0:T(8,128)(2,1)S(1)}, u32[]{:S(2)}, u32[]{:S(2)}) async-start(bf16[32,56,128]{2,1,0:T(8,128)(2,1)} %bitcast.29), calls=%async_computation | async-start | bytes 917504 | tf_op jit(solution)/shard_map/all_to_all | solution.py:361
  55.3 0.9 collective-permute-start.4
  56.3 1.5 %collective-permute-start.3 = (bf16[2,224,128]{2,1,0:T(8,128)(2,1)S(1)}, bf16[2,224,128]{2,1,0:T(8,128)(2,1)S(1)}, u32[]{:S(2)}, u32[]{:S(2)}) collective-permute-start(bf16[2,224,128]{2,1,0:T(8,128)(2,1)S(1)} %slice_bitcast_fusion.1), channel_id=1, source_target_pairs={{0,64},{32,96},{64,128},{96,160},{128,192},{160,224},{192,0},{224,... | collective-permute-start | bytes 344072 | tf_op jit(solution)/shard_map/ppermute | solution.py:325
  57.8 4.8 %collective-permute-done.3 = bf16[2,224,128]{2,1,0:T(8,128)(2,1)S(1)} collective-permute-done((bf16[2,224,128]{2,1,0:T(8,128)(2,1)S(1)}, bf16[2,224,128]{2,1,0:T(8,128)(2,1)S(1)}, u32[]{:S(2)}, u32[]{:S(2)}) %collective-permute-start.3) | collective-permute-done | bytes 114720 | tf_op jit(solution)/shard_map/ppermute | solution.py:325
  62.7 8.9 %all-to-all-done = bf16[32,56,128]{2,1,0:T(8,128)(2,1)S(1)} async-done(((bf16[32,56,128]{2,1,0:T(8,128)(2,1)}), bf16[32,56,128]{2,1,0:T(8,128)(2,1)S(1)}, u32[]{:S(2)}, u32[]{:S(2)}) %all-to-all-start) | async-done | bytes 458784 | tf_op jit(solution)/shard_map/all_to_all | solution.py:361
  71.6 0.7 copy-done.1
  72.3 11.1 %stats.1 = (f32[8,4,1792]{2,1,0:T(4,128)}, bf16[1792,128]{1,0:T(8,128)(2,1)}, bf16[128,1792]{1,0:T(8,128)(2,1)}, bf16[128,1792]{1,0:T(8,128)(2,1)}) custom-call(bf16[8,2,224,128]{3,2,1,0:T(8,128)(2,1)} %copy-done, s32[1]{0:T(128)} %bitcast.8.refs_1_, bf16[1792,128]{1,0:T(8,128)(2,1)} %bitcast.26, bf16[224,128]{1,0:T(8,128)(2,1)} %refs_3_.1, ...), custom_call_target="tpu_custom_call" | custom-call | tf_op jit(solution)/shard_map/stats/pallas_call | solution.py:184
  83.4 14.8 %all_to_all.15.part_ref = f32[8,4,1792]{2,1,0:T(4,128)} all-to-all(f32[8,4,1792]{2,1,0:T(4,128)} %get-tuple-element.19), channel_id=1, replica_groups=mesh['x'=4,'y'=2,'z'=8,'height'=4] {'z'}, dimensions={0} | all-to-all | bytes 458752 | tf_op jit(solution)/shard_map/all_to_all | solution.py:364
  98.2 19.2 %grads.1 = (bf16[2,224,128]{2,1,0:T(8,128)(2,1)}, bf16[2,224,128]{2,1,0:T(8,128)(2,1)}, bf16[2,224,128]{2,1,0:T(8,128)(2,1)}, bf16[2,224,128]{2,1,0:T(8,128)(2,1...) custom-call(bf16[8,2,224,128]{3,2,1,0:T(8,128)(2,1)} %copy-done, ...), custom_call_target="tpu_custom_call" | custom-call | tf_op jit(solution)/shard_map/grads/pallas_call | solution.py:279
  117.5 3.5 %all-to-all-start.2 = ((bf16[8,224,128]{2,1,0:T(8,128)(2,1)}), bf16[8,224,128]{2,1,0:T(8,128)(2,1)S(1)}, u32[]{:S(2)}, u32[]{:S(2)}) async-start(bf16[8,224,128]{2,1,0:T(8,128)(2,1)} %bitcast.31), calls=%async_computation.2 | async-start | bytes 917504 | tf_op jit(solution)/shard_map/all_to_all | solution.py:366
  120.9 0.8 collective-permute-start.16
  121.8 0.8 collective-permute-start.17
  122.6 1.2 collective-permute-start.18
  123.8 1.5 %collective-permute-start.19 = (bf16[2,224,128]{2,1,0:T(8,128)(2,1)}, bf16[2,224,128]{2,1,0:T(8,128)(2,1)S(1)}, u32[]{:S(2)}, u32[]{:S(2)}) collective-permute-start(bf16[2,224,128]{2,1,0:T(8,128)(2,1)} %get-tuple-element.25), channel_id=1, source_target_pairs={{0,64},{32,96},{64,128},{96,160},{128,192},{160,224},{192,0},{224,... | collective-permute-start | bytes 344072 | tf_op jit(solution)/shard_map/ppermute | solution.py:325
  125.3 1.4 collective-permute-start.20
  126.7 2.0 %collective-permute-start.21 = (bf16[2,224,128]{2,1,0:T(8,128)(2,1)}, bf16[2,224,128]{2,1,0:T(8,128)(2,1)S(1)}, u32[]{:S(2)}, u32[]{:S(2)}) collective-permute-start(bf16[2,224,128]{2,1,0:T(8,128)(2,1)} %get-tuple-element.27), channel_id=1, source_target_pairs={{0,128},{32,160},{64,192},{96,224},{128,0},{160,32},{192,64},{224,... | collective-permute-start | bytes 344072 | tf_op jit(solution)/shard_map/ppermute | solution.py:325
  128.7 2.2 %collective-permute-start.22 = (bf16[2,224,128]{2,1,0:T(8,128)(2,1)}, bf16[2,224,128]{2,1,0:T(8,128)(2,1)S(1)}, u32[]{:S(2)}, u32[]{:S(2)}) collective-permute-start(bf16[2,224,128]{2,1,0:T(8,128)(2,1)} %get-tuple-element.28), channel_id=1, source_target_pairs={{0,160},{32,128},{64,224},{96,192},{128,32},{160,0},{192,96},{224,... | collective-permute-start | bytes 344072 | tf_op jit(solution)/shard_map/ppermute | solution.py:325
  131.0 3.6 %collective-permute-done.20 = bf16[2,224,128]{2,1,0:T(8,128)(2,1)S(1)} collective-permute-done((bf16[2,224,128]{2,1,0:T(8,128)(2,1)}, bf16[2,224,128]{2,1,0:T(8,128)(2,1)S(1)}, u32[]{:S(2)}, u32[]{:S(2)}) %collective-permute-start.20) | collective-permute-done | bytes 114720 | tf_op jit(solution)/shard_map/ppermute | solution.py:325
  134.6 1.5 %collective-permute-done.22 = bf16[2,224,128]{2,1,0:T(8,128)(2,1)S(1)} collective-permute-done((bf16[2,224,128]{2,1,0:T(8,128)(2,1)}, bf16[2,224,128]{2,1,0:T(8,128)(2,1)S(1)}, u32[]{:S(2)}, u32[]{:S(2)}) %collective-permute-start.22) | collective-permute-done | bytes 114720 | tf_op jit(solution)/shard_map/ppermute | solution.py:325
  136.1 1.0 add_convert_fusion
  137.2 0.6 slice_bitcast_fusion.2
  137.8 0.7 reduce_sum.12
  (53 shorter events, 0.3 us)
Async XLA Ops:
  0.6 19.6 %collective-permute-start.9 = (bf16[224,128]{1,0:T(8,128)(2,1)}, bf16[224,128]{1,0:T(8,128)(2,1)S(1)}, u32[]{:S(2)}, u32[]{:S(2)}) collective-permute-start(bf16[224,128]{1,0:T(8,128)(2,1)} %refs_3_.1), channel_id=1, source_target_pairs={{0,4},{4,8},{8,12},{12,16},{16,20},{20,24},{24,28},{28,0},{1,5},{5... | collective-permute-start | bytes 172040 | tf_op jit(solution)/shard_map/ppermute | solution.py:305
  2.6 17.7 %collective-permute-start.13 = (bf16[224,128]{1,0:T(8,128)(2,1)}, bf16[224,128]{1,0:T(8,128)(2,1)S(1)}, u32[]{:S(2)}, u32[]{:S(2)}) collective-permute-start(bf16[224,128]{1,0:T(8,128)(2,1)} %refs_3_.1), channel_id=1, source_target_pairs={{0,28},{4,0},{8,4},{12,8},{16,12},{20,16},{24,20},{28,24},{1,29},{... | collective-permute-start | bytes 172040 | tf_op jit(solution)/shard_map/ppermute | solution.py:305
  7.5 16.9 %collective-permute-start = (bf16[2,224,128]{2,1,0:T(8,128)(2,1)S(1)}, bf16[2,224,128]{2,1,0:T(8,128)(2,1)S(1)}, u32[]{:S(2)}, u32[]{:S(2)}) collective-permute-start(bf16[2,224,128]{2,1,0:T(8,128)(2,1)S(1)} %get-tuple-element.36), channel_id=1, source_target_pairs={{0,32},{32,0},{64,96},{96,64},{128,160},{160,128},{192,224},{224,1... | collective-permute-start | bytes 344072 | tf_op jit(solution)/shard_map/ppermute | solution.py:325
  9.9 17.5 %collective-permute-start.6 = (bf16[1,4,56,256]{3,2,1,0:T(8,128)(2,1)S(1)}, bf16[1,4,56,256]{3,2,1,0:T(8,128)(2,1)S(1)}, u32[]{:S(2)}, u32[]{:S(2)}) collective-permute-start(bf16[1,4,56,256]{3,2,1,0:T(8,128)(2,1)S(1)} %get-tuple-element.31), channel_id=1, source_target_pairs={{4,0},{8,4},{12,8},{16,12},{20,16},{24,20},{28,24},{32,28},{36,32}... | collective-permute-start | bytes 344072 | tf_op jit(solution)/shard_map/ppermute | solution.py:30
  11.2 16.1 %collective-permute-start.5 = (bf16[1,4,56,256]{3,2,1,0:T(8,128)(2,1)S(1)}, bf16[1,4,56,256]{3,2,1,0:T(8,128)(2,1)S(1)}, u32[]{:S(2)}, u32[]{:S(2)}) collective-permute-start(bf16[1,4,56,256]{3,2,1,0:T(8,128)(2,1)S(1)} %get-tuple-element.32), channel_id=1, source_target_pairs={{0,4},{4,8},{8,12},{12,16},{16,20},{20,24},{24,28},{28,32},{32,36}... | collective-permute-start | bytes 344072 | tf_op jit(solution)/shard_map/ppermute | solution.py:29
  16.6 10.7 %copy-start.2 = (bf16[2,4,56,256]{3,2,1,0:T(8,128)(2,1)S(1)}, bf16[2,4,56,256]{3,2,1,0:T(8,128)(2,1)}, u32[]{:S(2)}) copy-start(bf16[2,4,56,256]{3,2,1,0:T(8,128)(2,1)} %own_ref.1) | copy-start | bytes 688132
  20.3 27.0 %copy-start.7 = (bf16[224,128]{1,0:T(8,128)(2,1)}, bf16[224,128]{1,0:T(8,128)(2,1)S(1)}, u32[]{:S(2)}) copy-start(bf16[224,128]{1,0:T(8,128)(2,1)S(1)} %collective-permute-done.9.refs_4_) | copy-start | bytes 172036
  20.3 11.5 %collective-permute-start.10 = (bf16[224,128]{1,0:T(8,128)(2,1)S(1)}, bf16[224,128]{1,0:T(8,128)(2,1)S(1)}, u32[]{:S(2)}, u32[]{:S(2)}) collective-permute-start(bf16[224,128]{1,0:T(8,128)(2,1)S(1)} %collective-permute-done.9.refs_4_), channel_id=1, source_target_pairs={{0,4},{4,8},{8,12},{12,16},{16,20},{20,24},{24,28},{28,0},{1,5},{5... | collective-permute-start | bytes 172040 | tf_op jit(solution)/shard_map/ppermute | solution.py:305
  20.3 27.0 %copy-start.8 = (bf16[224,128]{1,0:T(8,128)(2,1)}, bf16[224,128]{1,0:T(8,128)(2,1)S(1)}, u32[]{:S(2)}) copy-start(bf16[224,128]{1,0:T(8,128)(2,1)S(1)} %collective-permute-done.13.refs_10_) | copy-start | bytes 172036
  20.3 11.6 %collective-permute-start.14 = (bf16[224,128]{1,0:T(8,128)(2,1)S(1)}, bf16[224,128]{1,0:T(8,128)(2,1)S(1)}, u32[]{:S(2)}, u32[]{:S(2)}) collective-permute-start(bf16[224,128]{1,0:T(8,128)(2,1)S(1)} %collective-permute-done.13.refs_10_), channel_id=1, source_target_pairs={{0,28},{4,0},{8,4},{12,8},{16,12},{20,16},{24,20},{28,24},{1,29},{... | collective-permute-start | bytes 172040 | tf_op jit(solution)/shard_map/ppermute | solution.py:305
  24.4 30.9 %collective-permute-start.2 = (bf16[2,2,224,128]{3,2,1,0:T(8,128)(2,1)S(1)}, bf16[2,2,224,128]{3,2,1,0:T(8,128)(2,1)S(1)}, u32[]{:S(2)}, u32[]{:S(2)}) collective-permute-start(bf16[2,2,224,128]{3,2,1,0:T(8,128)(2,1)S(1)} %pad_maximum_fusion), channel_id=1, source_target_pairs={{0,192},{32,224},{64,0},{96,32},{128,64},{160,96},{192,128},{224,1... | collective-permute-start | bytes 688136 | tf_op jit(solution)/shard_map/ppermute | solution.py:325
  27.3 12.0 %copy-start.4 = (bf16[1,4,56,256]{3,2,1,0:T(8,128)(2,1)}, bf16[1,4,56,256]{3,2,1,0:T(8,128)(2,1)S(1)}, u32[]{:S(2)}) copy-start(bf16[1,4,56,256]{3,2,1,0:T(8,128)(2,1)S(1)} %collective-permute-done.5.before_ref) | copy-start | bytes 344068
  27.3 11.9 %copy-start.3 = (bf16[1,4,56,256]{3,2,1,0:T(8,128)(2,1)}, bf16[1,4,56,256]{3,2,1,0:T(8,128)(2,1)S(1)}, u32[]{:S(2)}) copy-start(bf16[1,4,56,256]{3,2,1,0:T(8,128)(2,1)S(1)} %collective-permute-done.6.after_ref) | copy-start | bytes 344068
  27.4 10.6 %collective-permute-start.8 = (bf16[4,1,56,256]{3,2,1,0:T(8,128)(2,1)S(1)}, bf16[4,1,56,256]{3,2,1,0:T(8,128)(2,1)S(1)}, u32[]{:S(2)}, u32[]{:S(2)}) collective-permute-start(bf16[4,1,56,256]{3,2,1,0:T(8,128)(2,1)S(1)} %get-tuple-element.29), channel_id=1, source_target_pairs={{1,0},{2,1},{3,2},{5,4},{6,5},{7,6},{9,8},{10,9},{11,10},{13,12},{... | collective-permute-start | bytes 344072 | tf_op jit(solution)/shard_map/ppermute | solution.py:30
  29.3 9.9 %collective-permute-start.7 = (bf16[4,1,56,256]{3,2,1,0:T(8,128)(2,1)S(1)}, bf16[4,1,56,256]{3,2,1,0:T(8,128)(2,1)S(1)}, u32[]{:S(2)}, u32[]{:S(2)}) collective-permute-start(bf16[4,1,56,256]{3,2,1,0:T(8,128)(2,1)S(1)} %get-tuple-element.30), channel_id=1, source_target_pairs={{0,1},{1,2},{2,3},{4,5},{5,6},{6,7},{8,9},{9,10},{10,11},{12,13},{... | collective-permute-start | bytes 344072 | tf_op jit(solution)/shard_map/ppermute | solution.py:29
  31.8 15.6 %copy-start.9 = (bf16[224,128]{1,0:T(8,128)(2,1)}, bf16[224,128]{1,0:T(8,128)(2,1)S(1)}, u32[]{:S(2)}) copy-start(bf16[224,128]{1,0:T(8,128)(2,1)S(1)} %collective-permute-done.10.refs_5_) | copy-start | bytes 172036
  31.8 5.5 %collective-permute-start.11 = (bf16[224,128]{1,0:T(8,128)(2,1)S(1)}, bf16[224,128]{1,0:T(8,128)(2,1)S(1)}, u32[]{:S(2)}, u32[]{:S(2)}) collective-permute-start(bf16[224,128]{1,0:T(8,128)(2,1)S(1)} %collective-permute-done.10.refs_5_), channel_id=1, source_target_pairs={{0,4},{4,8},{8,12},{12,16},{16,20},{20,24},{24,28},{28,0},{1,5},{5... | collective-permute-start | bytes 172040 | tf_op jit(solution)/shard_map/ppermute | solution.py:305
  31.9 39.7 %copy-start.10 = (bf16[224,128]{1,0:T(8,128)(2,1)}, bf16[224,128]{1,0:T(8,128)(2,1)S(1)}, u32[]{:S(2)}) copy-start(bf16[224,128]{1,0:T(8,128)(2,1)S(1)} %collective-permute-done.14.refs_9_) | copy-start | bytes 172036
  31.9 24.3 %collective-permute-start.1 = (bf16[2,2,224,128]{3,2,1,0:T(8,128)(2,1)S(1)}, bf16[2,2,224,128]{3,2,1,0:T(8,128)(2,1)S(1)}, u32[]{:S(2)}, u32[]{:S(2)}) collective-permute-start(bf16[2,2,224,128]{3,2,1,0:T(8,128)(2,1)S(1)} %pad_maximum_fusion), channel_id=1, source_target_pairs={{0,64},{32,96},{64,128},{96,160},{128,192},{160,224},{192,0},{224,... | collective-permute-start | bytes 688136 | tf_op jit(solution)/shard_map/ppermute | solution.py:325
  37.2 34.4 %copy-start.11 = (bf16[224,128]{1,0:T(8,128)(2,1)}, bf16[224,128]{1,0:T(8,128)(2,1)S(1)}, u32[]{:S(2)}) copy-start(bf16[224,128]{1,0:T(8,128)(2,1)S(1)} %collective-permute-done.11.refs_6_) | copy-start | bytes 172036
  37.2 25.5 %collective-permute-start.15 = (bf16[224,128]{1,0:T(8,128)(2,1)S(1)}, bf16[224,128]{1,0:T(8,128)(2,1)S(1)}, u32[]{:S(2)}, u32[]{:S(2)}) collective-permute-start(bf16[224,128]{1,0:T(8,128)(2,1)S(1)} %collective-permute-done.14.refs_9_), channel_id=1, source_target_pairs={{0,28},{4,0},{8,4},{12,8},{16,12},{20,16},{24,20},{28,24},{1,29},{... | collective-permute-start | bytes 172040 | tf_op jit(solution)/shard_map/ppermute | solution.py:305
  38.0 1.3 copy-start.5
  38.0 24.7 %collective-permute-start.12 = (bf16[224,128]{1,0:T(8,128)(2,1)S(1)}, bf16[224,128]{1,0:T(8,128)(2,1)S(1)}, u32[]{:S(2)}, u32[]{:S(2)}) collective-permute-start(bf16[224,128]{1,0:T(8,128)(2,1)S(1)} %collective-permute-done.11.refs_6_), channel_id=1, source_target_pairs={{0,4},{4,8},{8,12},{12,16},{16,20},{20,24},{24,28},{28,0},{1,5},{5... | collective-permute-start | bytes 172040 | tf_op jit(solution)/shard_map/ppermute | solution.py:305
  39.3 0.6 copy-start.6
  47.3 24.3 %all-to-all-start = ((bf16[32,56,128]{2,1,0:T(8,128)(2,1)}), bf16[32,56,128]{2,1,0:T(8,128)(2,1)S(1)}, u32[]{:S(2)}, u32[]{:S(2)}) async-start(bf16[32,56,128]{2,1,0:T(8,128)(2,1)} %bitcast.29), calls=%async_computation | async-start | bytes 917504 | tf_op jit(solution)/shard_map/all_to_all | solution.py:361
  55.3 7.3 %collective-permute-start.4 = (bf16[2,224,128]{2,1,0:T(8,128)(2,1)S(1)}, bf16[2,224,128]{2,1,0:T(8,128)(2,1)S(1)}, u32[]{:S(2)}, u32[]{:S(2)}) collective-permute-start(bf16[2,224,128]{2,1,0:T(8,128)(2,1)S(1)} %slice_bitcast_fusion), channel_id=1, source_target_pairs={{0,192},{32,224},{64,0},{96,32},{128,64},{160,96},{192,128},{224,1... | collective-permute-start | bytes 344072 | tf_op jit(solution)/shard_map/ppermute | solution.py:325
  56.3 6.4 %collective-permute-start.3 = (bf16[2,224,128]{2,1,0:T(8,128)(2,1)S(1)}, bf16[2,224,128]{2,1,0:T(8,128)(2,1)S(1)}, u32[]{:S(2)}, u32[]{:S(2)}) collective-permute-start(bf16[2,224,128]{2,1,0:T(8,128)(2,1)S(1)} %slice_bitcast_fusion.1), channel_id=1, source_target_pairs={{0,64},{32,96},{64,128},{96,160},{128,192},{160,224},{192,0},{224,... | collective-permute-start | bytes 344072 | tf_op jit(solution)/shard_map/ppermute | solution.py:325
  62.7 8.9 %copy-start = (bf16[8,2,224,128]{3,2,1,0:T(8,128)(2,1)}, bf16[8,2,224,128]{3,2,1,0:T(8,128)(2,1)S(1)}, u32[]{:S(2)}) copy-start(bf16[8,2,224,128]{3,2,1,0:T(8,128)(2,1)S(1)} %bitcast_dynamic-update-slice_fusion.refs_0_.kv_ref) | copy-start | bytes 2752516
  62.7 8.9 %copy-start.12 = (bf16[224,128]{1,0:T(8,128)(2,1)}, bf16[224,128]{1,0:T(8,128)(2,1)S(1)}, u32[]{:S(2)}) copy-start(bf16[224,128]{1,0:T(8,128)(2,1)S(1)} %collective-permute-done.15.refs_8_) | copy-start | bytes 172036
  62.7 8.9 %copy-start.13 = (bf16[224,128]{1,0:T(8,128)(2,1)}, bf16[224,128]{1,0:T(8,128)(2,1)S(1)}, u32[]{:S(2)}) copy-start(bf16[224,128]{1,0:T(8,128)(2,1)S(1)} %collective-permute-done.12.refs_7_) | copy-start | bytes 172036
  71.6 0.8 copy-start.1
  117.5 20.4 %all-to-all-start.2 = ((bf16[8,224,128]{2,1,0:T(8,128)(2,1)}), bf16[8,224,128]{2,1,0:T(8,128)(2,1)S(1)}, u32[]{:S(2)}, u32[]{:S(2)}) async-start(bf16[8,224,128]{2,1,0:T(8,128)(2,1)} %bitcast.31), calls=%async_computation.2 | async-start | bytes 917504 | tf_op jit(solution)/shard_map/all_to_all | solution.py:366
  120.9 5.8 %collective-permute-start.16 = (bf16[2,224,128]{2,1,0:T(8,128)(2,1)}, bf16[2,224,128]{2,1,0:T(8,128)(2,1)S(1)}, u32[]{:S(2)}, u32[]{:S(2)}) collective-permute-start(bf16[2,224,128]{2,1,0:T(8,128)(2,1)} %get-tuple-element.22), channel_id=1, source_target_pairs={{0,32},{32,0},{64,96},{96,64},{128,160},{160,128},{192,224},{224,1... | collective-permute-start | bytes 344072 | tf_op jit(solution)/shard_map/ppermute | solution.py:325
  121.8 7.0 %collective-permute-start.17 = (bf16[2,224,128]{2,1,0:T(8,128)(2,1)}, bf16[2,224,128]{2,1,0:T(8,128)(2,1)S(1)}, u32[]{:S(2)}, u32[]{:S(2)}) collective-permute-start(bf16[2,224,128]{2,1,0:T(8,128)(2,1)} %get-tuple-element.23), channel_id=1, source_target_pairs={{0,192},{32,224},{64,0},{96,32},{128,64},{160,96},{192,128},{224,1... | collective-permute-start | bytes 344072 | tf_op jit(solution)/shard_map/ppermute | solution.py:325
  122.6 8.4 %collective-permute-start.18 = (bf16[2,224,128]{2,1,0:T(8,128)(2,1)}, bf16[2,224,128]{2,1,0:T(8,128)(2,1)S(1)}, u32[]{:S(2)}, u32[]{:S(2)}) collective-permute-start(bf16[2,224,128]{2,1,0:T(8,128)(2,1)} %get-tuple-element.24), channel_id=1, source_target_pairs={{0,224},{32,192},{64,32},{96,0},{128,96},{160,64},{192,160},{224,1... | collective-permute-start | bytes 344072 | tf_op jit(solution)/shard_map/ppermute | solution.py:325
  123.8 7.1 %collective-permute-start.19 = (bf16[2,224,128]{2,1,0:T(8,128)(2,1)}, bf16[2,224,128]{2,1,0:T(8,128)(2,1)S(1)}, u32[]{:S(2)}, u32[]{:S(2)}) collective-permute-start(bf16[2,224,128]{2,1,0:T(8,128)(2,1)} %get-tuple-element.25), channel_id=1, source_target_pairs={{0,64},{32,96},{64,128},{96,160},{128,192},{160,224},{192,0},{224,... | collective-permute-start | bytes 344072 | tf_op jit(solution)/shard_map/ppermute | solution.py:325
  125.3 9.3 %collective-permute-start.20 = (bf16[2,224,128]{2,1,0:T(8,128)(2,1)}, bf16[2,224,128]{2,1,0:T(8,128)(2,1)S(1)}, u32[]{:S(2)}, u32[]{:S(2)}) collective-permute-start(bf16[2,224,128]{2,1,0:T(8,128)(2,1)} %get-tuple-element.26), channel_id=1, source_target_pairs={{0,96},{32,64},{64,160},{96,128},{128,224},{160,192},{192,32},{224... | collective-permute-start | bytes 344072 | tf_op jit(solution)/shard_map/ppermute | solution.py:325
  126.7 7.9 %collective-permute-start.21 = (bf16[2,224,128]{2,1,0:T(8,128)(2,1)}, bf16[2,224,128]{2,1,0:T(8,128)(2,1)S(1)}, u32[]{:S(2)}, u32[]{:S(2)}) collective-permute-start(bf16[2,224,128]{2,1,0:T(8,128)(2,1)} %get-tuple-element.27), channel_id=1, source_target_pairs={{0,128},{32,160},{64,192},{96,224},{128,0},{160,32},{192,64},{224,... | collective-permute-start | bytes 344072 | tf_op jit(solution)/shard_map/ppermute | solution.py:325
  128.7 7.4 %collective-permute-start.22 = (bf16[2,224,128]{2,1,0:T(8,128)(2,1)}, bf16[2,224,128]{2,1,0:T(8,128)(2,1)S(1)}, u32[]{:S(2)}, u32[]{:S(2)}) collective-permute-start(bf16[2,224,128]{2,1,0:T(8,128)(2,1)} %get-tuple-element.28), channel_id=1, source_target_pairs={{0,160},{32,128},{64,224},{96,192},{128,32},{160,0},{192,96},{224,... | collective-permute-start | bytes 344072 | tf_op jit(solution)/shard_map/ppermute | solution.py:325

commit v4 on v2

--- a/solution.py
+++ b/solution.py
@@ -18,6 +18,7 @@
 DEPTH = ("x", "y", "z")
 SPAN = 64
 TILE = 256
+GROUP = 2
 
 
 def halo_pair(block, axis, dim):
@@ -190,7 +191,8 @@
 def grads_body(kv_ref, q_ref, g_ref, qt_ref, gt_ref, part_ref, *rest):
     dkv_refs, (dq_ref, p_ref, s_ref, acc_ref, st_ref) = (rest[:-5], rest[-5:])
     block = pl.program_id(0)
-    rows = kv_ref.shape[2]
+    group, _, per_shard, _ = kv_ref.shape
+    rows = group * per_shard
     count, width = q_ref.shape
 
     @pl.when(block == 0)
@@ -205,8 +207,8 @@
             st_ref[2 * head + 1 : 2 * head + 2, :] = delta / total
         acc_ref[...] = jnp.zeros_like(acc_ref)
 
-    keys = kv_ref[0, 0]
-    values = kv_ref[0, 1]
+    keys = kv_ref[:, 0].reshape(rows, width)
+    values = kv_ref[:, 1].reshape(rows, width)
     keys_t = keys.T
     head_of = lax.broadcasted_iota(jnp.int32, (rows, width), 1) // HSZ
     dks = []
@@ -236,10 +238,12 @@
     dv = dv.astype(jnp.bfloat16)
     for shard, dkv_ref in enumerate(dkv_refs):
 
-        @pl.when(block == shard)
-        def _(dkv_ref=dkv_ref):
-            dkv_ref[0] = dk
-            dkv_ref[1] = dv
+        span = slice(shard % group * per_shard, (shard % group + 1) * per_shard)
+
+        @pl.when(block == shard // group)
+        def _(dkv_ref=dkv_ref, span=span):
+            dkv_ref[0] = dk[span]
+            dkv_ref[1] = dv[span]
 
     @pl.when(block == pl.num_programs(0) - 1)
     def _():
@@ -256,9 +260,9 @@
 
     return pl.pallas_call(
         grads_body,
-        grid=(shards,),
+        grid=(shards // GROUP,),
         in_specs=[
-            pl.BlockSpec((1, 2, rows, width), lambda i: (i, 0, 0, 0)),
+            pl.BlockSpec((GROUP, 2, rows, width), lambda i: (i, 0, 0, 0)),
             whole(query_count, width),
             whole(query_count, width),
             whole(width, query_count),
@@ -269,8 +273,8 @@
         out_shape=[jax.ShapeDtypeStruct((2, rows, width), jnp.bfloat16)] * shards
         + [jax.ShapeDtypeStruct((query_count, width), jnp.bfloat16)],
         scratch_shapes=[
-            pltpu.VMEM((heads, rows, query_count), jnp.bfloat16),
-            pltpu.VMEM((heads, rows, query_count), jnp.bfloat16),
+            pltpu.VMEM((heads, GROUP * rows, query_count), jnp.bfloat16),
+            pltpu.VMEM((heads, GROUP * rows, query_count), jnp.bfloat16),
             pltpu.VMEM((width, query_count), jnp.float32),
             pltpu.VMEM((2 * heads, query_count), jnp.float32),
         ],

time: 142 us -> 141 us (level)
  no operation moved by 1% of the time
where the time goes in v4:
time: 141 us; the launch traced here: 140 us
  starting transfers between devices  55 us (39%)
  Pallas kernels  37.4 us (27%)
  waiting for transfers between devices  21.8 us (15%)
  blocking collectives  14.8 us (10%)
  local copies, waits for them, and re-layouts  6.97 us (5%)
  other arithmetic  2.76 us (2%)
    pallas_call x1, Pallas kernels, local_grads(): pl.pallas_call(grads_body, grid=(shards // GROUP,), in_specs=[pl.BlockSpe...  19.2 us
    ppermute x12, starting transfers between devices, moved(): return lax.ppermute(array, KEY_AXES, pairs)  18.5 us
    all_to_all x1, blocking collectives, body(): parts = lax.all_to_all(part, QUERY_AXIS, 0, 0, tiled=True)  14.8 us
    pallas_call x1, Pallas kernels, local_stats(): pl.pallas_call(lambda *refs: stats_body(*refs, rows=112), grid=(query_cou...  10.8 us
    all_to_all x1, waiting for transfers between devices, body(): every_grad = lax.all_to_all(apart, (QUERY_AXIS, 'height'), 0, 0, tiled=True)  10.5 us
    all_to_all x1, starting transfers between devices, body(): every_grad = lax.all_to_all(apart, (QUERY_AXIS, 'height'), 0, 0, tiled=True)  10.5 us
    all_to_all x1, starting transfers between devices, spread_to(): return lax.all_to_all(copies, axes, 0, 0, tiled=True)  10.4 us
    ppermute x12, waiting for transfers between devices, moved(): return lax.ppermute(array, KEY_AXES, pairs)  8.95 us
  transfers between devices with their start and end apart: 19, of which 9 were waited for; matrix products, arithmetic and copies ran while one was open for 5% of the time, Pallas kernels for 5%

profile of v4, /device:TPU:16, one launch (start us, length us, event | category | flops | bytes accessed | tf_op | source)
XLA Modules:
  0.0 139.7 jit_solution(8439757245927096895)
XLA Ops:
  0.6 1.0 fusion
  1.7 1.4 collective-permute-start
  3.0 1.0 fusion.2
  4.0 3.8 %collective-permute-start.5 = (bf16[1,4,56,256]{3,2,1,0:T(8,128)(2,1)S(1)}, bf16[1,4,56,256]{3,2,1,0:T(8,128)(2,1)S(1)}, u32[]{:S(2)}, u32[]{:S(2)}) collective-permute-start(bf16[1,4,56,256]{3,2,1,0:T(8,128)(2,1)S(1)} %get-tuple-element.30), channel_id=1, source_target_pairs={{0,4},{4,8},{8,12},{12,16},{16,20},{20,24},{24,28},{28,32},{32,36}... | collective-permute-start | bytes 344072 | tf_op jit(solution)/shard_map/ppermute | solution.py:29
  7.8 1.3 collective-permute-start.6
  9.1 1.7 %broadcast_in_dim.2 = bf16[8,224,128]{2,1,0:T(8,128)(2,1)} broadcast(bf16[224,128]{1,0:T(8,128)(2,1)} %param.6), dimensions={1,2} | broadcast | bytes 516096 | tf_op jit(solution)/shard_map/broadcast_in_dim | solution.py:287
  10.8 10.4 %all-to-all-start = ((bf16[8,224,128]{2,1,0:T(8,128)(2,1)}), bf16[8,224,128]{2,1,0:T(8,128)(2,1)S(1)}, u32[]{:S(2)}, u32[]{:S(2)}) async-start(bf16[8,224,128]{2,1,0:T(8,128)(2,1)} %broadcast_in_dim.2), calls=%async_computation | async-start | bytes 917504 | tf_op jit(solution)/shard_map/all_to_all | solution.py:288
  21.2 0.0 copy-start.7
  21.2 0.0 copy-start.8
  21.2 0.0 copy-start.4
  21.2 2.0 %copy.9 = bf16[64,8,8,256]{3,1,2,0:T(8,128)(2,1)} copy(bf16[64,8,8,256]{3,2,1,0:T(8,128)(2,1)S(1)} %bitcast.30) | data formatting | bytes 4194304
  23.3 0.0 collective-permute-done
  23.3 1.6 %collective-permute-start.1 = (bf16[2,2,224,128]{3,2,1,0:T(8,128)(2,1)S(1)}, bf16[2,2,224,128]{3,2,1,0:T(8,128)(2,1)S(1)}, u32[]{:S(2)}, u32[]{:S(2)}) collective-permute-start(bf16[2,2,224,128]{3,2,1,0:T(8,128)(2,1)S(1)} %pad_maximum_fusion), channel_id=1, source_target_pairs={{0,64},{32,96},{64,128},{96,160},{128,192},{160,224},{192,0},{224,... | collective-permute-start | bytes 688136 | tf_op jit(solution)/shard_map/ppermute | solution.py:298
  24.9 1.7 %collective-permute-start.2 = (bf16[2,2,224,128]{3,2,1,0:T(8,128)(2,1)S(1)}, bf16[2,2,224,128]{3,2,1,0:T(8,128)(2,1)S(1)}, u32[]{:S(2)}, u32[]{:S(2)}) collective-permute-start(bf16[2,2,224,128]{3,2,1,0:T(8,128)(2,1)S(1)} %pad_maximum_fusion), channel_id=1, source_target_pairs={{0,192},{32,224},{64,0},{96,32},{128,64},{160,96},{192,128},{224,1... | collective-permute-start | bytes 688136 | tf_op jit(solution)/shard_map/ppermute | solution.py:298
  26.8 1.9 %collective-permute-start.7 = (bf16[4,1,56,256]{3,2,1,0:T(8,128)(2,1)S(1)}, bf16[4,1,56,256]{3,2,1,0:T(8,128)(2,1)S(1)}, u32[]{:S(2)}, u32[]{:S(2)}) collective-permute-start(bf16[4,1,56,256]{3,2,1,0:T(8,128)(2,1)S(1)} %get-tuple-element.28), channel_id=1, source_target_pairs={{0,1},{1,2},{2,3},{4,5},{5,6},{6,7},{8,9},{9,10},{10,11},{12,13},{... | collective-permute-start | bytes 344072 | tf_op jit(solution)/shard_map/ppermute | solution.py:29
  28.7 5.1 %collective-permute-start.8 = (bf16[4,1,56,256]{3,2,1,0:T(8,128)(2,1)S(1)}, bf16[4,1,56,256]{3,2,1,0:T(8,128)(2,1)S(1)}, u32[]{:S(2)}, u32[]{:S(2)}) collective-permute-start(bf16[4,1,56,256]{3,2,1,0:T(8,128)(2,1)S(1)} %get-tuple-element.27), channel_id=1, source_target_pairs={{1,0},{2,1},{3,2},{5,4},{6,5},{7,6},{9,8},{10,9},{11,10},{13,12},{... | collective-permute-start | bytes 344072 | tf_op jit(solution)/shard_map/ppermute | solution.py:30
  33.9 0.5 collective-permute-done.7.above_ref
  34.4 1.8 %collective-permute-done.8.below_ref = bf16[4,1,56,256]{3,2,1,0:T(8,128)(2,1)S(1)} collective-permute-done((bf16[4,1,56,256]{3,2,1,0:T(8,128)(2,1)S(1)}, bf16[4,1,56,256]{3,2,1,0:T(8,128)(2,1)S(1)}, u32[]{:S(2)}, u32[]{:S(2)}) %collective-permute-start.8) | collective-permute-done | bytes 114720 | tf_op jit(solution)/shard_map/ppermute | solution.py:30
  36.2 0.6 copy-done.10
  36.8 7.4 %conv.1 = bf16[8,4,56,128]{3,2,1,0:T(8,128)(2,1)} custom-call(bf16[2,4,56,256]{3,2,1,0:T(8,128)(2,1)} %own_ref.1, bf16[1,4,56,256]{3,2,1,0:T(8,128)(2,1)} %copy-done.5, bf16[1,4,56,256]{3,2,1,0:T(8,128)(2,1)} %copy-done.6, bf16[4,1,56,256]{3,2,1,0:T(8,128)(2,1)} %copy-done.9, bf16[4,1,56,256]{3,2,1,0:T(8,128)(2,1)} %copy-done.10, ...), custom_call_target="tpu_custom_call" | custom-call | tf_op jit(solution)/shard_map/conv/pallas_call | solution.py:114
  44.2 0.4 collective-permute-start.3
  44.6 10.5 %all-to-all-start.1 = ((bf16[32,56,128]{2,1,0:T(8,128)(2,1)}), bf16[32,56,128]{2,1,0:T(8,128)(2,1)S(1)}, u32[]{:S(2)}, u32[]{:S(2)}) async-start(bf16[32,56,128]{2,1,0:T(8,128)(2,1)} %bitcast.31), calls=%async_computation.1 | async-start | bytes 917504 | tf_op jit(solution)/shard_map/all_to_all | solution.py:334
  55.1 0.0 collective-permute-done.2
  55.1 3.0 %collective-permute-start.4 = (bf16[2,224,128]{2,1,0:T(8,128)(2,1)S(1)}, bf16[2,224,128]{2,1,0:T(8,128)(2,1)S(1)}, u32[]{:S(2)}, u32[]{:S(2)}) collective-permute-start(bf16[2,224,128]{2,1,0:T(8,128)(2,1)S(1)} %slice_bitcast_fusion), channel_id=1, source_target_pairs={{0,192},{32,224},{64,0},{96,32},{128,64},{160,96},{192,128},{224,1... | collective-permute-start | bytes 344072 | tf_op jit(solution)/shard_map/ppermute | solution.py:298
  58.2 0.0 collective-permute-done.3
  58.2 2.6 %collective-permute-done.4 = bf16[2,224,128]{2,1,0:T(8,128)(2,1)S(1)} collective-permute-done((bf16[2,224,128]{2,1,0:T(8,128)(2,1)S(1)}, bf16[2,224,128]{2,1,0:T(8,128)(2,1)S(1)}, u32[]{:S(2)}, u32[]{:S(2)}) %collective-permute-start.4) | collective-permute-done | bytes 114720 | tf_op jit(solution)/shard_map/ppermute | solution.py:298
  60.8 10.5 %all-to-all-done.1 = bf16[32,56,128]{2,1,0:T(8,128)(2,1)S(1)} async-done(((bf16[32,56,128]{2,1,0:T(8,128)(2,1)}), bf16[32,56,128]{2,1,0:T(8,128)(2,1)S(1)}, u32[]{:S(2)}, u32[]{:S(2)}) %all-to-all-start.1) | async-done | bytes 458784 | tf_op jit(solution)/shard_map/all_to_all | solution.py:334
  71.3 0.8 copy-done.2
  72.1 10.8 %stats.1 = (f32[8,4,1792]{2,1,0:T(4,128)}, bf16[128,1792]{1,0:T(8,128)(2,1)}, bf16[128,1792]{1,0:T(8,128)(2,1)}) custom-call(bf16[8,2,224,128]{3,2,1,0:T(8,128)(2,1)} %copy-done, bf16[1792,128]{1,0:T(8,128)(2,1)} %bitcast.26, bf16[1792,128]{1,0:T(8,128)(2,1)} %bitcast.28), custom_call_target="tpu_custom_call" | custom-call | tf_op jit(solution)/shard_map/stats/pallas_call | solution.py:173
  82.9 14.8 %all_to_all.20.part_ref = f32[8,4,1792]{2,1,0:T(4,128)} all-to-all(f32[8,4,1792]{2,1,0:T(4,128)} %get-tuple-element.17), channel_id=1, replica_groups=mesh['x'=4,'y'=2,'z'=8,'height'=4] {'z'}, dimensions={0} | all-to-all | bytes 458752 | tf_op jit(solution)/shard_map/all_to_all | solution.py:337
  97.8 19.2 %grads.1 = (bf16[2,224,128]{2,1,0:T(8,128)(2,1)}, bf16[2,224,128]{2,1,0:T(8,128)(2,1)}, bf16[2,224,128]{2,1,0:T(8,128)(2,1)}, bf16[2,224,128]{2,1,0:T(8,128)(2,1...) custom-call(bf16[8,2,224,128]{3,2,1,0:T(8,128)(2,1)} %copy-done, ...), custom_call_target="tpu_custom_call" | custom-call | tf_op jit(solution)/shard_map/grads/pallas_call | solution.py:261
  117.0 3.5 %all-to-all-start.3 = ((bf16[8,224,128]{2,1,0:T(8,128)(2,1)}), bf16[8,224,128]{2,1,0:T(8,128)(2,1)S(1)}, u32[]{:S(2)}, u32[]{:S(2)}) async-start(bf16[8,224,128]{2,1,0:T(8,128)(2,1)} %bitcast.33), calls=%async_computation.3 | async-start | bytes 917504 | tf_op jit(solution)/shard_map/all_to_all | solution.py:339
  120.5 3.0 %collective-permute-start.10 = (bf16[2,224,128]{2,1,0:T(8,128)(2,1)}, bf16[2,224,128]{2,1,0:T(8,128)(2,1)S(1)}, u32[]{:S(2)}, u32[]{:S(2)}) collective-permute-start(bf16[2,224,128]{2,1,0:T(8,128)(2,1)} %get-tuple-element.21), channel_id=1, source_target_pairs={{0,192},{32,224},{64,0},{96,32},{128,64},{160,96},{192,128},{224,1... | collective-permute-start | bytes 344072 | tf_op jit(solution)/shard_map/ppermute | solution.py:298
  123.5 0.5 collective-permute-start.11
  124.0 1.7 %collective-permute-start.12 = (bf16[2,224,128]{2,1,0:T(8,128)(2,1)}, bf16[2,224,128]{2,1,0:T(8,128)(2,1)S(1)}, u32[]{:S(2)}, u32[]{:S(2)}) collective-permute-start(bf16[2,224,128]{2,1,0:T(8,128)(2,1)} %get-tuple-element.23), channel_id=1, source_target_pairs={{0,64},{32,96},{64,128},{96,160},{128,192},{160,224},{192,0},{224,... | collective-permute-start | bytes 344072 | tf_op jit(solution)/shard_map/ppermute | solution.py:298
  125.7 0.7 collective-permute-start.13
  126.4 3.0 %collective-permute-start.14 = (bf16[2,224,128]{2,1,0:T(8,128)(2,1)}, bf16[2,224,128]{2,1,0:T(8,128)(2,1)S(1)}, u32[]{:S(2)}, u32[]{:S(2)}) collective-permute-start(bf16[2,224,128]{2,1,0:T(8,128)(2,1)} %get-tuple-element.25), channel_id=1, source_target_pairs={{0,128},{32,160},{64,192},{96,224},{128,0},{160,32},{192,64},{224,... | collective-permute-start | bytes 344072 | tf_op jit(solution)/shard_map/ppermute | solution.py:298
  129.4 0.0 collective-permute-done.10
  129.4 0.7 collective-permute-start.15
  130.1 0.5 collective-permute-done.11
  130.6 0.8 collective-permute-start.9
  131.4 0.7 collective-permute-done.12
  132.1 3.2 %collective-permute-done.13 = bf16[2,224,128]{2,1,0:T(8,128)(2,1)S(1)} collective-permute-done((bf16[2,224,128]{2,1,0:T(8,128)(2,1)}, bf16[2,224,128]{2,1,0:T(8,128)(2,1)S(1)}, u32[]{:S(2)}, u32[]{:S(2)}) %collective-permute-start.13) | collective-permute-done | bytes 114720 | tf_op jit(solution)/shard_map/ppermute | solution.py:298
  135.3 1.5 %collective-permute-done.15 = bf16[2,224,128]{2,1,0:T(8,128)(2,1)S(1)} collective-permute-done((bf16[2,224,128]{2,1,0:T(8,128)(2,1)}, bf16[2,224,128]{2,1,0:T(8,128)(2,1)S(1)}, u32[]{:S(2)}, u32[]{:S(2)}) %collective-permute-start.15) | collective-permute-done | bytes 114720 | tf_op jit(solution)/shard_map/ppermute | solution.py:298
  136.8 0.5 collective-permute-done.9
  137.3 1.0 add_convert_fusion
  138.3 0.6 slice_bitcast_fusion.2
  139.0 0.7 reduce_sum.12
  (36 shorter events, 0.3 us)
Async XLA Ops:
  0.6 20.6 %copy-start.3 = (bf16[512,8,256]{2,1,0:T(8,128)(2,1)S(1)}, bf16[512,8,256]{2,1,0:T(8,128)(2,1)}, u32[]{:S(2)}) copy-start(bf16[512,8,256]{2,1,0:T(8,128)(2,1)} %param.11) | copy-start | bytes 6291460
  1.7 21.6 %collective-permute-start = (bf16[2,224,128]{2,1,0:T(8,128)(2,1)S(1)}, bf16[2,224,128]{2,1,0:T(8,128)(2,1)S(1)}, u32[]{:S(2)}, u32[]{:S(2)}) collective-permute-start(bf16[2,224,128]{2,1,0:T(8,128)(2,1)S(1)} %get-tuple-element.34), channel_id=1, source_target_pairs={{0,32},{32,0},{64,96},{96,64},{128,160},{160,128},{192,224},{224,1... | collective-permute-start | bytes 344072 | tf_op jit(solution)/shard_map/ppermute | solution.py:298
  4.0 22.7 %collective-permute-start.5 = (bf16[1,4,56,256]{3,2,1,0:T(8,128)(2,1)S(1)}, bf16[1,4,56,256]{3,2,1,0:T(8,128)(2,1)S(1)}, u32[]{:S(2)}, u32[]{:S(2)}) collective-permute-start(bf16[1,4,56,256]{3,2,1,0:T(8,128)(2,1)S(1)} %get-tuple-element.30), channel_id=1, source_target_pairs={{0,4},{4,8},{8,12},{12,16},{16,20},{20,24},{24,28},{28,32},{32,36}... | collective-permute-start | bytes 344072 | tf_op jit(solution)/shard_map/ppermute | solution.py:29
  7.8 18.9 %collective-permute-start.6 = (bf16[1,4,56,256]{3,2,1,0:T(8,128)(2,1)S(1)}, bf16[1,4,56,256]{3,2,1,0:T(8,128)(2,1)S(1)}, u32[]{:S(2)}, u32[]{:S(2)}) collective-permute-start(bf16[1,4,56,256]{3,2,1,0:T(8,128)(2,1)S(1)} %get-tuple-element.29), channel_id=1, source_target_pairs={{4,0},{8,4},{12,8},{16,12},{20,16},{24,20},{28,24},{32,28},{36,32}... | collective-permute-start | bytes 344072 | tf_op jit(solution)/shard_map/ppermute | solution.py:30
  10.8 33.8 %all-to-all-start = ((bf16[8,224,128]{2,1,0:T(8,128)(2,1)}), bf16[8,224,128]{2,1,0:T(8,128)(2,1)S(1)}, u32[]{:S(2)}, u32[]{:S(2)}) async-start(bf16[8,224,128]{2,1,0:T(8,128)(2,1)} %broadcast_in_dim.2), calls=%async_computation | async-start | bytes 917504 | tf_op jit(solution)/shard_map/all_to_all | solution.py:288
  21.2 2.1 %copy-start.7 = (bf16[224,128]{1,0:T(8,128)(2,1)S(1)}, bf16[224,128]{1,0:T(8,128)(2,1)}, u32[]{:S(2)}) copy-start(bf16[224,128]{1,0:T(8,128)(2,1)} %param.8) | copy-start | bytes 172036
  21.2 2.1 %copy-start.8 = (bf16[224,128]{1,0:T(8,128)(2,1)S(1)}, bf16[224,128]{1,0:T(8,128)(2,1)}, u32[]{:S(2)}) copy-start(bf16[224,128]{1,0:T(8,128)(2,1)} %param.7) | copy-start | bytes 172036
  21.2 5.4 %copy-start.4 = (bf16[2,4,56,256]{3,2,1,0:T(8,128)(2,1)S(1)}, bf16[2,4,56,256]{3,2,1,0:T(8,128)(2,1)}, u32[]{:S(2)}) copy-start(bf16[2,4,56,256]{3,2,1,0:T(8,128)(2,1)} %own_ref.1) | copy-start | bytes 688132
  23.3 20.9 %collective-permute-start.1 = (bf16[2,2,224,128]{3,2,1,0:T(8,128)(2,1)S(1)}, bf16[2,2,224,128]{3,2,1,0:T(8,128)(2,1)S(1)}, u32[]{:S(2)}, u32[]{:S(2)}) collective-permute-start(bf16[2,2,224,128]{3,2,1,0:T(8,128)(2,1)S(1)} %pad_maximum_fusion), channel_id=1, source_target_pairs={{0,64},{32,96},{64,128},{96,160},{128,192},{160,224},{192,0},{224,... | collective-permute-start | bytes 688136 | tf_op jit(solution)/shard_map/ppermute | solution.py:298
  24.9 30.2 %collective-permute-start.2 = (bf16[2,2,224,128]{3,2,1,0:T(8,128)(2,1)S(1)}, bf16[2,2,224,128]{3,2,1,0:T(8,128)(2,1)S(1)}, u32[]{:S(2)}, u32[]{:S(2)}) collective-permute-start(bf16[2,2,224,128]{3,2,1,0:T(8,128)(2,1)S(1)} %pad_maximum_fusion), channel_id=1, source_target_pairs={{0,192},{32,224},{64,0},{96,32},{128,64},{160,96},{192,128},{224,1... | collective-permute-start | bytes 688136 | tf_op jit(solution)/shard_map/ppermute | solution.py:298
  26.7 9.5 %copy-start.5 = (bf16[1,4,56,256]{3,2,1,0:T(8,128)(2,1)}, bf16[1,4,56,256]{3,2,1,0:T(8,128)(2,1)S(1)}, u32[]{:S(2)}) copy-start(bf16[1,4,56,256]{3,2,1,0:T(8,128)(2,1)S(1)} %collective-permute-done.5.before_ref) | copy-start | bytes 344068
  26.7 9.5 %copy-start.6 = (bf16[1,4,56,256]{3,2,1,0:T(8,128)(2,1)}, bf16[1,4,56,256]{3,2,1,0:T(8,128)(2,1)S(1)}, u32[]{:S(2)}) copy-start(bf16[1,4,56,256]{3,2,1,0:T(8,128)(2,1)S(1)} %collective-permute-done.6.after_ref) | copy-start | bytes 344068
  26.8 7.6 %collective-permute-start.7 = (bf16[4,1,56,256]{3,2,1,0:T(8,128)(2,1)S(1)}, bf16[4,1,56,256]{3,2,1,0:T(8,128)(2,1)S(1)}, u32[]{:S(2)}, u32[]{:S(2)}) collective-permute-start(bf16[4,1,56,256]{3,2,1,0:T(8,128)(2,1)S(1)} %get-tuple-element.28), channel_id=1, source_target_pairs={{0,1},{1,2},{2,3},{4,5},{5,6},{6,7},{8,9},{9,10},{10,11},{12,13},{... | collective-permute-start | bytes 344072 | tf_op jit(solution)/shard_map/ppermute | solution.py:29
  28.7 7.5 %collective-permute-start.8 = (bf16[4,1,56,256]{3,2,1,0:T(8,128)(2,1)S(1)}, bf16[4,1,56,256]{3,2,1,0:T(8,128)(2,1)S(1)}, u32[]{:S(2)}, u32[]{:S(2)}) collective-permute-start(bf16[4,1,56,256]{3,2,1,0:T(8,128)(2,1)S(1)} %get-tuple-element.27), channel_id=1, source_target_pairs={{1,0},{2,1},{3,2},{5,4},{6,5},{7,6},{9,8},{10,9},{11,10},{13,12},{... | collective-permute-start | bytes 344072 | tf_op jit(solution)/shard_map/ppermute | solution.py:30
  34.4 1.8 %copy-start.9 = (bf16[4,1,56,256]{3,2,1,0:T(8,128)(2,1)}, bf16[4,1,56,256]{3,2,1,0:T(8,128)(2,1)S(1)}, u32[]{:S(2)}) copy-start(bf16[4,1,56,256]{3,2,1,0:T(8,128)(2,1)S(1)} %collective-permute-done.7.above_ref) | copy-start | bytes 344068
  36.2 0.6 copy-start.10
  44.2 13.9 %collective-permute-start.3 = (bf16[2,224,128]{2,1,0:T(8,128)(2,1)S(1)}, bf16[2,224,128]{2,1,0:T(8,128)(2,1)S(1)}, u32[]{:S(2)}, u32[]{:S(2)}) collective-permute-start(bf16[2,224,128]{2,1,0:T(8,128)(2,1)S(1)} %slice_bitcast_fusion.1), channel_id=1, source_target_pairs={{0,64},{32,96},{64,128},{96,160},{128,192},{160,224},{192,0},{224,... | collective-permute-start | bytes 344072 | tf_op jit(solution)/shard_map/ppermute | solution.py:298
  44.6 26.7 %copy-start.1 = (bf16[8,224,128]{2,1,0:T(8,128)(2,1)}, bf16[8,224,128]{2,1,0:T(8,128)(2,1)S(1)}, u32[]{:S(2)}) copy-start(bf16[8,224,128]{2,1,0:T(8,128)(2,1)S(1)} %all-to-all-done) | copy-start | bytes 1376260
  44.6 26.7 %all-to-all-start.1 = ((bf16[32,56,128]{2,1,0:T(8,128)(2,1)}), bf16[32,56,128]{2,1,0:T(8,128)(2,1)S(1)}, u32[]{:S(2)}, u32[]{:S(2)}) async-start(bf16[32,56,128]{2,1,0:T(8,128)(2,1)} %bitcast.31), calls=%async_computation.1 | async-start | bytes 917504 | tf_op jit(solution)/shard_map/all_to_all | solution.py:334
  55.1 5.7 %collective-permute-start.4 = (bf16[2,224,128]{2,1,0:T(8,128)(2,1)S(1)}, bf16[2,224,128]{2,1,0:T(8,128)(2,1)S(1)}, u32[]{:S(2)}, u32[]{:S(2)}) collective-permute-start(bf16[2,224,128]{2,1,0:T(8,128)(2,1)S(1)} %slice_bitcast_fusion), channel_id=1, source_target_pairs={{0,192},{32,224},{64,0},{96,32},{128,64},{160,96},{192,128},{224,1... | collective-permute-start | bytes 344072 | tf_op jit(solution)/shard_map/ppermute | solution.py:298
  60.8 10.5 %copy-start = (bf16[8,2,224,128]{3,2,1,0:T(8,128)(2,1)}, bf16[8,2,224,128]{3,2,1,0:T(8,128)(2,1)S(1)}, u32[]{:S(2)}) copy-start(bf16[8,2,224,128]{3,2,1,0:T(8,128)(2,1)S(1)} %bitcast_dynamic-update-slice_fusion.refs_0_.kv_ref) | copy-start | bytes 2752516
  71.3 0.8 copy-start.2
  117.0 22.0 %all-to-all-start.3 = ((bf16[8,224,128]{2,1,0:T(8,128)(2,1)}), bf16[8,224,128]{2,1,0:T(8,128)(2,1)S(1)}, u32[]{:S(2)}, u32[]{:S(2)}) async-start(bf16[8,224,128]{2,1,0:T(8,128)(2,1)} %bitcast.33), calls=%async_computation.3 | async-start | bytes 917504 | tf_op jit(solution)/shard_map/all_to_all | solution.py:339
  120.5 8.9 %collective-permute-start.10 = (bf16[2,224,128]{2,1,0:T(8,128)(2,1)}, bf16[2,224,128]{2,1,0:T(8,128)(2,1)S(1)}, u32[]{:S(2)}, u32[]{:S(2)}) collective-permute-start(bf16[2,224,128]{2,1,0:T(8,128)(2,1)} %get-tuple-element.21), channel_id=1, source_target_pairs={{0,192},{32,224},{64,0},{96,32},{128,64},{160,96},{192,128},{224,1... | collective-permute-start | bytes 344072 | tf_op jit(solution)/shard_map/ppermute | solution.py:298
  123.5 7.1 %collective-permute-start.11 = (bf16[2,224,128]{2,1,0:T(8,128)(2,1)}, bf16[2,224,128]{2,1,0:T(8,128)(2,1)S(1)}, u32[]{:S(2)}, u32[]{:S(2)}) collective-permute-start(bf16[2,224,128]{2,1,0:T(8,128)(2,1)} %get-tuple-element.22), channel_id=1, source_target_pairs={{0,224},{32,192},{64,32},{96,0},{128,96},{160,64},{192,160},{224,1... | collective-permute-start | bytes 344072 | tf_op jit(solution)/shard_map/ppermute | solution.py:298
  124.0 8.1 %collective-permute-start.12 = (bf16[2,224,128]{2,1,0:T(8,128)(2,1)}, bf16[2,224,128]{2,1,0:T(8,128)(2,1)S(1)}, u32[]{:S(2)}, u32[]{:S(2)}) collective-permute-start(bf16[2,224,128]{2,1,0:T(8,128)(2,1)} %get-tuple-element.23), channel_id=1, source_target_pairs={{0,64},{32,96},{64,128},{96,160},{128,192},{160,224},{192,0},{224,... | collective-permute-start | bytes 344072 | tf_op jit(solution)/shard_map/ppermute | solution.py:298
  125.7 9.7 %collective-permute-start.13 = (bf16[2,224,128]{2,1,0:T(8,128)(2,1)}, bf16[2,224,128]{2,1,0:T(8,128)(2,1)S(1)}, u32[]{:S(2)}, u32[]{:S(2)}) collective-permute-start(bf16[2,224,128]{2,1,0:T(8,128)(2,1)} %get-tuple-element.24), channel_id=1, source_target_pairs={{0,96},{32,64},{64,160},{96,128},{128,224},{160,192},{192,32},{224... | collective-permute-start | bytes 344072 | tf_op jit(solution)/shard_map/ppermute | solution.py:298
  126.4 8.9 %collective-permute-start.14 = (bf16[2,224,128]{2,1,0:T(8,128)(2,1)}, bf16[2,224,128]{2,1,0:T(8,128)(2,1)S(1)}, u32[]{:S(2)}, u32[]{:S(2)}) collective-permute-start(bf16[2,224,128]{2,1,0:T(8,128)(2,1)} %get-tuple-element.25), channel_id=1, source_target_pairs={{0,128},{32,160},{64,192},{96,224},{128,0},{160,32},{192,64},{224,... | collective-permute-start | bytes 344072 | tf_op jit(solution)/shard_map/ppermute | solution.py:298
  129.4 7.4 %collective-permute-start.15 = (bf16[2,224,128]{2,1,0:T(8,128)(2,1)}, bf16[2,224,128]{2,1,0:T(8,128)(2,1)S(1)}, u32[]{:S(2)}, u32[]{:S(2)}) collective-permute-start(bf16[2,224,128]{2,1,0:T(8,128)(2,1)} %get-tuple-element.26), channel_id=1, source_target_pairs={{0,160},{32,128},{64,224},{96,192},{128,32},{160,0},{192,96},{224,... | collective-permute-start | bytes 344072 | tf_op jit(solution)/shard_map/ppermute | solution.py:298
  130.6 6.7 %collective-permute-start.9 = (bf16[2,224,128]{2,1,0:T(8,128)(2,1)}, bf16[2,224,128]{2,1,0:T(8,128)(2,1)S(1)}, u32[]{:S(2)}, u32[]{:S(2)}) collective-permute-start(bf16[2,224,128]{2,1,0:T(8,128)(2,1)} %get-tuple-element.20), channel_id=1, source_target_pairs={{0,32},{32,0},{64,96},{96,64},{128,160},{160,128},{192,224},{224,1... | collective-permute-start | bytes 344072 | tf_op jit(solution)/shard_map/ppermute | solution.py:298
